TPU v7x, 32 devices: a whole 2x2x4 slice. The times are simulated.
32 devices in a mesh: graph: 8 (over y, x, core), tm: 4 (over z).
Axes of the slice: x: 2, y: 2, z: 4, core: 2. Of those that a mesh axis runs over, the one named last changes fastest.
Arguments:
- series: bfloat16 [16, 32, 4096], P('tm', None, 'graph'), may hold values from -6 to 6
- convolution_weight: bfloat16 [2, 2, 64, 32], replicated, may hold values from -0.75 to 0.75
- convolution_bias: float32 [2, 64], replicated, may hold values from -3 to 3
- mixing_weight: bfloat16 [2, 5, 32, 32], replicated, may hold values from -0.5 to 0.5
- mix_bias: float32 [2, 32], replicated, may hold values from -3 to 3
- tile_values: bfloat16 [32, 3, 128, 128], P('graph'), may hold values from -0.3125 to 0.3125
- tile_cols: int32 [32, 3], P('graph'), may hold values from 0 to 5
- send_index: int32 [8, 8, 32], P('graph'), may hold values from 0 to 511
- send_mask: int32 [8, 8, 32], P('graph'), may hold values 0 or 1
- cotangent: bfloat16 [16, 32, 4096], P('tm', None, 'graph'), may hold values from -6 to 6
Outputs:
- output: bfloat16 [16, 32, 4096], P('tm', None, 'graph')
- grad_series: bfloat16 [16, 32, 4096], P('tm', None, 'graph')
- grad_conv: float32 [2, 2, 64, 32], replicated
- grad_mix: float32 [2, 5, 32, 32], replicated
Inputs may be any that keep to these rules, and one draw needn't show every extreme that they name: `send_index`: a local sensor number of the sending partition; a list may name a sensor more than once. `tile_cols`: blocks below 4 are the partition's own sensors, the others its boundary rows.
All inputs are finite; a program needn't handle non-finite values. No bound on the sum of `send_mask` on one device may be relied on, other than what follows from the above.
Results may differ from a plain program's by a relative error of at most 0.0079.
Values may be sent and summed in bfloat16 or wider, within the bound.
A program may use at most 64 MiB of HBM per device.

v0:
```python
import math

import jax
import jax.numpy as jnp
from jax import lax
from jax.sharding import PartitionSpec as P

GATED_LAYERS = 2


def from_behind(x, axis, by):
    size = lax.axis_size(axis)
    pairs = [(i, i + by) for i in range(size) if 0 <= i + by < size]
    return lax.ppermute(x, axis, pairs)


def apply_tiles(extended, columns, values):
    height = extended.shape[0]
    tile_width = values.shape[-1]
    blocks = extended.reshape(height, -1, tile_width)
    result = None
    for tile_slot in range(columns.shape[1]):
        picked = jnp.take(blocks, columns[:, tile_slot], axis=1)
        tile_term = jnp.einsum(
            "mrj,rij->mri", picked, values[:, tile_slot], preferred_element_type=jnp.float32
        )
        result = tile_term if result is None else result + tile_term
    return result.reshape(height, -1)


def gather_rows(signal, tables):
    indices, live_half, live_full, columns, values = tables
    return jnp.take(signal, indices, axis=1) * live_half[None, :]


def finish_pull(signal, received, tables):
    indices, live_half, live_full, columns, values = tables
    extended = jnp.concatenate([signal, received], axis=1)
    return apply_tiles(extended, columns, values)


def start_push(signal, tables):
    indices, live_half, live_full, columns, values = tables
    height, sensor_count = signal.shape
    tile_width = values.shape[-1]
    col_count = (sensor_count + indices.shape[0]) // tile_width
    blocks = signal.reshape(height, columns.shape[0], tile_width)
    totals = jnp.zeros((height, col_count, tile_width), jnp.float32)
    for tile_slot in range(columns.shape[1]):
        contrib = jnp.einsum(
            "mri,rij->mrj", blocks, values[:, tile_slot], preferred_element_type=jnp.float32
        )
        totals = totals.at[:, columns[:, tile_slot]].add(contrib)
    totals = totals.reshape(height, -1)
    return (totals[:, :sensor_count], totals[:, sensor_count:].astype(jnp.bfloat16))


def finish_push(local_part, returned, tables):
    indices, live_half, live_full, columns, values = tables
    return local_part.at[:, indices].add(returned.astype(jnp.float32) * live_full[None, :])


def pull_hop(signal, tables):
    received = lax.all_to_all(
        gather_rows(signal, tables), "graph", split_axis=1, concat_axis=1, tiled=True
    )
    return finish_pull(signal, received, tables)


def push_hop(signal, tables):
    local_part, outgoing = start_push(signal, tables)
    returned = lax.all_to_all(outgoing, "graph", split_axis=1, concat_axis=1, tiled=True)
    return finish_push(local_part, returned, tables)


def hop_pair(pull_in, push_in, tables):
    return (pull_hop(pull_in, tables), push_hop(push_in, tables))


def channel_mix(matrix, signal):
    return jnp.einsum("oc,tcn->ton", matrix, signal, preferred_element_type=jnp.float32)


def channel_back(matrix, signal):
    return jnp.einsum("oc,ton->tcn", matrix, signal, preferred_element_type=jnp.float32)


def outer_sum(left_side, right_side):
    return jnp.einsum("ton,tcn->oc", left_side, right_side, preferred_element_type=jnp.float32)


def per_device(
    series,
    convolution_weight,
    convolution_bias,
    mixing_weight,
    mix_bias,
    tile_values,
    tile_cols,
    send_index,
    send_mask,
    cotangent,
):
    steps, res_count, sensors = series.shape
    dilation_count = convolution_weight.shape[2] // 2
    live_full = send_mask.reshape(-1).astype(jnp.float32)
    tables = (
        send_index.reshape(-1),
        live_full.astype(jnp.bfloat16),
        live_full,
        tile_cols,
        tile_values,
    )

    def graph_pair(pull_in, push_in):
        shape_in = pull_in.shape
        pulled, pushed = hop_pair(
            pull_in.reshape(-1, sensors), push_in.reshape(-1, sensors), tables
        )
        return (pulled.reshape(shape_in), pushed.reshape(shape_in))

    hidden = series
    saved = []
    for layer_index in range(GATED_LAYERS):
        dilation = layer_index + 1
        previous = from_behind(hidden[steps - dilation :], "tm", 1)
        lagged = jnp.concatenate([previous, hidden[: steps - dilation]], axis=0)
        preactivation = channel_mix(convolution_weight[layer_index, 0], hidden) + channel_mix(
            convolution_weight[layer_index, 1], lagged
        )
        preactivation = preactivation + convolution_bias[layer_index][None, :, None]
        filter_half = jnp.tanh(preactivation[:, :dilation_count])
        gate_half = jax.nn.sigmoid(preactivation[:, dilation_count:])
        gated = (filter_half * gate_half).astype(jnp.bfloat16)
        fwd_one, back_one = graph_pair(gated, gated)
        fwd_one = fwd_one.astype(jnp.bfloat16)
        back_one = back_one.astype(jnp.bfloat16)
        fwd_two, back_two = graph_pair(fwd_one, back_one)
        hop_list = (
            gated,
            fwd_one,
            fwd_two.astype(jnp.bfloat16),
            back_one,
            back_two.astype(jnp.bfloat16),
        )
        mixed_sum = mix_bias[layer_index][None, :, None] + channel_mix(
            mixing_weight[layer_index, 0], hop_list[0]
        )
        for hop_order in range(1, 5):
            mixed_sum = mixed_sum + channel_mix(
                mixing_weight[layer_index, hop_order], hop_list[hop_order]
            )
        saved.append((hidden, lagged, filter_half, gate_half, hop_list))
        hidden = (hidden.astype(jnp.float32) + mixed_sum).astype(jnp.bfloat16)
    grad_flow = cotangent.astype(jnp.float32)
    conv_list = [None] * GATED_LAYERS
    mix_list = [None] * GATED_LAYERS
    for layer_index in reversed(range(GATED_LAYERS)):
        dilation = layer_index + 1
        layer_input, lagged, filter_half, gate_half, hop_list = saved[layer_index]
        flow_round = grad_flow.astype(jnp.bfloat16)
        mix_here = jnp.stack([outer_sum(flow_round, hop_list[hop_order]) for hop_order in range(5)])
        hop_grads = [
            channel_back(mixing_weight[layer_index, hop_order], flow_round)
            for hop_order in range(5)
        ]
        back_inner, fwd_inner = graph_pair(
            hop_grads[4].astype(jnp.bfloat16), hop_grads[2].astype(jnp.bfloat16)
        )
        back_outer, fwd_outer = graph_pair(
            (hop_grads[3] + back_inner).astype(jnp.bfloat16),
            (hop_grads[1] + fwd_inner).astype(jnp.bfloat16),
        )
        grad_gated = hop_grads[0] + fwd_outer + back_outer
        grad_filter = grad_gated * gate_half * (1.0 - filter_half * filter_half)
        grad_gate = grad_gated * filter_half * gate_half * (1.0 - gate_half)
        grad_pre = jnp.concatenate([grad_filter, grad_gate], axis=1).astype(jnp.bfloat16)
        conv_here = jnp.stack([outer_sum(grad_pre, layer_input), outer_sum(grad_pre, lagged)])
        lag_term = channel_back(convolution_weight[layer_index, 1], grad_pre)
        tail_term = from_behind(lag_term[:dilation].astype(jnp.bfloat16), "tm", -1).astype(
            jnp.float32
        )
        lag_rest = lag_term[dilation:]
        grad_flow = (
            grad_flow
            + channel_back(convolution_weight[layer_index, 0], grad_pre)
            + jnp.concatenate([lag_rest, tail_term], axis=0)
        )
        conv_list[layer_index] = conv_here
        mix_list[layer_index] = mix_here
    conv_all = jnp.stack(conv_list)
    mix_all = jnp.stack(mix_list)
    conv_all, mix_all = lax.psum((conv_all, mix_all), ("graph", "tm"))
    norm_scale = 1.0 / math.sqrt(
        float(steps * lax.axis_size("tm") * sensors * lax.axis_size("graph"))
    )
    return (hidden, grad_flow.astype(jnp.bfloat16), conv_all * norm_scale, mix_all * norm_scale)


def solution(mesh):
    return jax.shard_map(
        per_device,
        mesh=mesh,
        in_specs=(
            P("tm", None, "graph"),
            P(),
            P(),
            P(),
            P(),
            P("graph", None, None, None),
            P("graph", None),
            P("graph", None, None),
            P("graph", None, None),
            P("tm", None, "graph"),
        ),
        out_specs=(P("tm", None, "graph"), P("tm", None, "graph"), P(), P()),
        check_vma=False,
    )
```

profile of v0, /device:TPU:0, one launch (start us, length us, event | category | flops | bytes accessed | tf_op | source)
XLA Modules:
  0.0 399.0 jit_solution(13689258011795526480)
XLA Ops:
  7.2 1.2 fusion.36
  12.8 5.3 %all-to-all-start.8 = ((bf16[128,8,32]{0,2,1:T(8,128)(2,1)}), bf16[128,8,32]{0,2,1:T(8,128)(2,1)S(1)}, u32[]{:S(2)}, u32[]{:S(2)}) async-start(bf16[128,8,32]{0,2,1:T(8,128)(2,1)} %bitcast.107), calls=%async_computation.8 | async-start | bytes 131072 | tf_op jit(solution)/shard_map/all_to_all | solution.py:72
  18.1 3.5 collective-permute-start
  21.8 0.9 convolution_convert_fusion.2
  36.2 4.2 %all-to-all-start = ((bf16[128,8,32]{0,2,1:T(8,128)(2,1)}), bf16[128,8,32]{0,2,1:T(8,128)(2,1)S(1)}, u32[]{:S(2)}, u32[]{:S(2)}) async-start(bf16[128,8,32]{0,2,1:T(8,128)(2,1)} %bitcast.11), calls=%async_computation | async-start | bytes 131072 | tf_op jit(solution)/shard_map/all_to_all | solution.py:64
  40.3 2.1 scatter_custom_fusion.19
  42.6 0.9 fusion.23
  47.3 4.2 %all-to-all-start.10 = ((bf16[128,8,32]{0,2,1:T(8,128)(2,1)}), bf16[128,8,32]{0,2,1:T(8,128)(2,1)S(1)}, u32[]{:S(2)}, u32[]{:S(2)}) async-start(bf16[128,8,32]{0,2,1:T(8,128)(2,1)} %bitcast.123), calls=%async_computation.10 | async-start | bytes 131072 | tf_op jit(solution)/shard_map/all_to_all | solution.py:64
  51.5 5.0 %all-to-all-done.10 = bf16[128,8,32]{0,2,1:T(8,128)(2,1)S(1)} async-done(((bf16[128,8,32]{0,2,1:T(8,128)(2,1)}), bf16[128,8,32]{0,2,1:T(8,128)(2,1)S(1)}, u32[]{:S(2)}, u32[]{:S(2)}) %all-to-all-start.10) | async-done | bytes 65568 | tf_op jit(solution)/shard_map/all_to_all | solution.py:64
  56.5 3.3 all-to-all-start.2
  60.6 1.2 gather_fusion.2
  63.3 1.3 gather_fusion.3
  64.7 1.3 gather_fusion.19
  66.0 4.1 %all-to-all-start.9 = ((bf16[128,8,32]{0,2,1:T(8,128)(2,1)}), bf16[128,8,32]{0,2,1:T(8,128)(2,1)}, u32[]{:S(2)}, u32[]{:S(2)}) async-start(bf16[128,8,32]{0,2,1:T(8,128)(2,1)} %bitcast.112), calls=%async_computation.9 | async-start | bytes 131072 | tf_op jit(solution)/shard_map/all_to_all | solution.py:72
  70.1 2.3 scatter_custom_fusion.3
  75.5 1.6 gather_fusion.4
  79.1 0.9 fusion.24
  80.2 1.0 gather_fusion.20
  81.4 1.6 convolution_add_fusion.10
  83.8 4.5 %all-to-all-start.11 = ((bf16[128,8,32]{0,2,1:T(8,128)(2,1)}), bf16[128,8,32]{0,2,1:T(8,128)(2,1)S(1)}, u32[]{:S(2)}, u32[]{:S(2)}) async-start(bf16[128,8,32]{0,2,1:T(8,128)(2,1)} %bitcast.132), calls=%async_computation.11 | async-start | bytes 131072 | tf_op jit(solution)/shard_map/all_to_all | solution.py:64
  91.8 2.4 scatter_custom_fusion.23
  95.1 4.2 %all-to-all-start.1 = ((bf16[128,8,32]{0,2,1:T(8,128)(2,1)}), bf16[128,8,32]{0,2,1:T(8,128)(2,1)S(1)}, u32[]{:S(2)}, u32[]{:S(2)}) async-start(bf16[128,8,32]{0,2,1:T(8,128)(2,1)} %bitcast.26), calls=%async_computation.1 | async-start | bytes 131072 | tf_op jit(solution)/shard_map/all_to_all | solution.py:64
  100.5 3.9 all-to-all-done.1
  104.3 3.4 all-to-all-start.3
  107.7 1.3 gather_fusion.22
  112.6 2.3 scatter_custom_fusion.7
  120.1 3.6 collective-permute-start.1
  127.3 1.2 fusion.3
  128.5 1.0 multiply_convert_fusion.3
  135.8 1.3 collective-permute-start.2
  137.3 1.6 gather_fusion.8
  138.9 3.5 all-to-all-start.6
  143.1 1.6 convolution_add_fusion.6
  145.5 1.9 all-to-all-done.6
  147.4 2.3 scatter_custom_fusion.11
  149.7 1.0 fusion.118
  151.3 1.7 scatter_fusion.9
  156.0 13.9 %all-to-all-start.7 = ((bf16[128,8,32]{0,2,1:T(8,128)(2,1)}), bf16[128,8,32]{0,2,1:T(8,128)(2,1)}, u32[]{:S(2)}, u32[]{:S(2)}) async-start(bf16[128,8,32]{0,2,1:T(8,128)(2,1)} %bitcast.93), calls=%async_computation.7 | async-start | bytes 131072 | tf_op jit(solution)/shard_map/all_to_all | solution.py:72
  172.5 0.9 convolution_convert_fusion
  173.4 0.9 fusion.37
  174.4 0.9 fusion.108
  175.2 0.9 fusion.82
  180.9 3.9 all-to-all-start.14
  185.6 0.9 copy-done.7
  190.1 2.4 scatter_custom_fusion.15
  192.7 4.2 %all-to-all-start.12 = ((bf16[128,8,32]{0,2,1:T(8,128)(2,1)}), bf16[128,8,32]{0,2,1:T(8,128)(2,1)S(1)}, u32[]{:S(2)}, u32[]{:S(2)}) async-start(bf16[128,8,32]{0,2,1:T(8,128)(2,1)} %bitcast.150), calls=%async_computation.12 | async-start | bytes 131072 | tf_op jit(solution)/shard_map/all_to_all | solution.py:72
  199.2 2.7 all-to-all-done.12
  202.0 2.3 scatter_custom_fusion.27
  204.4 0.9 fusion.25
  205.3 0.9 fusion.106
  208.7 0.9 fusion.26
  211.4 3.4 all-to-all-start.4
  215.7 0.9 copy-done.6
  219.9 4.1 %all-to-all-start.15 = ((bf16[128,8,32]{0,2,1:T(8,128)(2,1)}), bf16[128,8,32]{0,2,1:T(8,128)(2,1)S(1)}, u32[]{:S(2)}, u32[]{:S(2)}) async-start(bf16[128,8,32]{0,2,1:T(8,128)(2,1)} %bitcast.175), calls=%async_computation.15 | async-start | bytes 131072 | tf_op jit(solution)/shard_map/all_to_all | solution.py:64
  224.0 5.0 %all-to-all-done.15 = bf16[128,8,32]{0,2,1:T(8,128)(2,1)S(1)} async-done(((bf16[128,8,32]{0,2,1:T(8,128)(2,1)}), bf16[128,8,32]{0,2,1:T(8,128)(2,1)S(1)}, u32[]{:S(2)}, u32[]{:S(2)}) %all-to-all-start.15) | async-done | bytes 65568 | tf_op jit(solution)/shard_map/all_to_all | solution.py:64
  229.0 3.4 all-to-all-start.13
  237.3 2.3 scatter_custom_fusion.31
  245.5 1.1 gather_fusion.12
  247.4 3.9 all-to-all-start.5
  251.3 1.3 collective-permute-start.3
  255.3 2.6 collective-permute-done.3
  262.8 1.6 pad_maximum_fusion.10
  265.2 124.5 %all-reduce.3.cloned.1.call-done = (f32[2,2,64,32]{2,3,1,0:T(8,128)}, f32[2,5,32,32]{3,2,1,0:T(8,128)}) async-done(((f32[2,2,64,32]{2,3,1,0:T(8,128)}, f32[2,5,32,32]{3,2,1,0:T(8,128)}), (f32[2,2,64,32]{2,3,1,0:T(8,128)}, f32[2,5,32,32]{3,2,1,0:T(8,128)})) %all-reduce.3.cloned.1.call-update) | async-done | bytes 73744 | tf_op jit(solution)/shard_map/psum | solution.py:193
  389.7 1.6 broadcast_multiply_fusion
  (407 shorter events, 101.8 us)
Async XLA Ops:
  7.2 1.2 copy-start
  12.1 6.0 %copy-start.2 = (bf16[4,32,512]{2,1,0:T(8,128)(2,1)S(1)}, bf16[4,32,512]{2,1,0:T(8,128)(2,1)}, u32[]{:S(2)}) copy-start(bf16[4,32,512]{2,1,0:T(8,128)(2,1)} %param.14) | copy-start | bytes 393220
  12.8 9.0 %copy-start.1 = (bf16[4,32,512]{2,1,0:T(8,128)(2,1)S(1)}, bf16[4,32,512]{2,1,0:T(8,128)(2,1)}, u32[]{:S(2)}) copy-start(bf16[4,32,512]{2,1,0:T(8,128)(2,1)} %param.23) | copy-start | bytes 393220
  12.8 23.4 %all-to-all-start.8 = ((bf16[128,8,32]{0,2,1:T(8,128)(2,1)}), bf16[128,8,32]{0,2,1:T(8,128)(2,1)S(1)}, u32[]{:S(2)}, u32[]{:S(2)}) async-start(bf16[128,8,32]{0,2,1:T(8,128)(2,1)} %bitcast.107), calls=%async_computation.8 | async-start | bytes 131072 | tf_op jit(solution)/shard_map/all_to_all | solution.py:72
  18.1 3.5 copy-start.58
  18.1 10.7 %collective-permute-start = (bf16[1,32,512]{2,1,0:T(8,128)(2,1)S(1)}, bf16[1,32,512]{2,1,0:T(8,128)(2,1)S(1)}, u32[]{:S(2)}, u32[]{:S(2)}) collective-permute-start(bf16[1,32,512]{2,1,0:T(8,128)(2,1)S(1)} %slice.116), channel_id=1, source_target_pairs={{0,1},{1,2},{2,3},{4,5},{5,6},{6,7},{8,9},{9,10},{10,11},{12,13},{... | collective-permute-start | bytes 98312 | tf_op jit(solution)/shard_map/ppermute | solution.py:14
  21.8 3.3 copy-start.28
  22.7 9.5 %copy-start.59 = (pred[256]{0:T(512)(128)(4,1)}, pred[256]{0:T(512)(128)(4,1)S(1)}, u32[]{:S(2)}) copy-start(pred[256]{0:T(512)(128)(4,1)S(1)} %compare_and_fusion.3) | copy-start | bytes 772
  24.6 15.7 %copy-start.72 = (s32[256,1]{0,1:T(1,128)}, s32[256,1]{0,1:T(1,128)S(1)}, u32[]{:S(2)}) copy-start(s32[256,1]{0,1:T(1,128)S(1)} %compare_select_fusion) | copy-start | bytes 3076
  26.4 4.1 %copy-start.46 = (s32[1024]{0:T(1024)}, s32[1024]{0:T(1024)S(1)}, u32[]{:S(2)}) copy-start(s32[1024]{0:T(1024)S(1)} %get-tuple-element.36) | copy-start | bytes 12292
  26.4 35.6 %copy-start.56 = (s32[1024]{0:T(1024)}, s32[1024]{0:T(1024)S(1)}, u32[]{:S(2)}) copy-start(s32[1024]{0:T(1024)S(1)} %get-tuple-element.35) | copy-start | bytes 12292
  27.0 33.6 %copy-start.57 = (s32[1024]{0:T(1024)}, s32[1024]{0:T(1024)S(1)}, u32[]{:S(2)}) copy-start(s32[1024]{0:T(1024)S(1)} %get-tuple-element.34) | copy-start | bytes 12292
  27.7 1.1 copy-start.18
  27.9 4.3 %copy-start.63 = (bf16[256]{0:T(256)(128)(2,1)}, bf16[256]{0:T(256)(128)(2,1)S(1)}, u32[]{:S(2)}) copy-start(bf16[256]{0:T(256)(128)(2,1)S(1)} %convert_element_type.244) | copy-start | bytes 1540
  36.2 11.1 %all-to-all-start = ((bf16[128,8,32]{0,2,1:T(8,128)(2,1)}), bf16[128,8,32]{0,2,1:T(8,128)(2,1)S(1)}, u32[]{:S(2)}, u32[]{:S(2)}) async-start(bf16[128,8,32]{0,2,1:T(8,128)(2,1)} %bitcast.11), calls=%async_computation | async-start | bytes 131072 | tf_op jit(solution)/shard_map/all_to_all | solution.py:64
  47.3 9.2 %all-to-all-start.10 = ((bf16[128,8,32]{0,2,1:T(8,128)(2,1)}), bf16[128,8,32]{0,2,1:T(8,128)(2,1)S(1)}, u32[]{:S(2)}, u32[]{:S(2)}) async-start(bf16[128,8,32]{0,2,1:T(8,128)(2,1)} %bitcast.123), calls=%async_computation.10 | async-start | bytes 131072 | tf_op jit(solution)/shard_map/all_to_all | solution.py:64
  56.5 9.5 %all-to-all-start.2 = ((bf16[128,8,32]{0,2,1:T(8,128)(2,1)}), bf16[128,8,32]{0,2,1:T(8,128)(2,1)S(1)}, u32[]{:S(2)}, u32[]{:S(2)}) async-start(bf16[128,8,32]{0,2,1:T(8,128)(2,1)} %bitcast.37), calls=%async_computation.2 | async-start | bytes 131072 | tf_op jit(solution)/shard_map/all_to_all | solution.py:72
  66.0 17.8 %all-to-all-start.9 = ((bf16[128,8,32]{0,2,1:T(8,128)(2,1)}), bf16[128,8,32]{0,2,1:T(8,128)(2,1)}, u32[]{:S(2)}, u32[]{:S(2)}) async-start(bf16[128,8,32]{0,2,1:T(8,128)(2,1)} %bitcast.112), calls=%async_computation.9 | async-start | bytes 131072 | tf_op jit(solution)/shard_map/all_to_all | solution.py:72
  73.4 0.9 copy-start.13
  74.3 0.9 copy-start.14
  75.5 1.6 copy-start.49
  77.7 0.9 copy-start.12
  77.7 0.9 copy-start.37
  81.4 1.6 copy-start.27
  81.4 1.6 copy-start.60
  81.4 1.6 copy-start.64
  83.8 11.3 %all-to-all-start.11 = ((bf16[128,8,32]{0,2,1:T(8,128)(2,1)}), bf16[128,8,32]{0,2,1:T(8,128)(2,1)S(1)}, u32[]{:S(2)}, u32[]{:S(2)}) async-start(bf16[128,8,32]{0,2,1:T(8,128)(2,1)} %bitcast.132), calls=%async_computation.11 | async-start | bytes 131072 | tf_op jit(solution)/shard_map/all_to_all | solution.py:64
  95.1 9.2 %all-to-all-start.1 = ((bf16[128,8,32]{0,2,1:T(8,128)(2,1)}), bf16[128,8,32]{0,2,1:T(8,128)(2,1)S(1)}, u32[]{:S(2)}, u32[]{:S(2)}) async-start(bf16[128,8,32]{0,2,1:T(8,128)(2,1)} %bitcast.26), calls=%async_computation.1 | async-start | bytes 131072 | tf_op jit(solution)/shard_map/all_to_all | solution.py:64
  104.3 8.3 %all-to-all-start.3 = ((bf16[128,8,32]{0,2,1:T(8,128)(2,1)}), bf16[128,8,32]{0,2,1:T(8,128)(2,1)S(1)}, u32[]{:S(2)}, u32[]{:S(2)}) async-start(bf16[128,8,32]{0,2,1:T(8,128)(2,1)} %bitcast.45), calls=%async_computation.3 | async-start | bytes 131072 | tf_op jit(solution)/shard_map/all_to_all | solution.py:72
  116.5 1.0 copy-start.9
  120.1 3.7 copy-start.11
  120.1 6.6 %copy-start.25 = (bf16[2,32,512]{2,1,0:T(8,128)(2,1)}, bf16[2,32,512]{2,1,0:T(8,128)(2,1)S(1)}, u32[]{:S(2)}) copy-start(bf16[2,32,512]{2,1,0:T(8,128)(2,1)S(1)} %get-tuple-element.20) | copy-start | bytes 196612
  120.1 5.9 %collective-permute-start.1 = (bf16[2,32,512]{2,1,0:T(8,128)(2,1)S(1)}, bf16[2,32,512]{2,1,0:T(8,128)(2,1)S(1)}, u32[]{:S(2)}, u32[]{:S(2)}) collective-permute-start(bf16[2,32,512]{2,1,0:T(8,128)(2,1)S(1)} %get-tuple-element.19), channel_id=1, source_target_pairs={{0,1},{1,2},{2,3},{4,5},{5,6},{6,7},{8,9},{9,10},{10,11},{12,13},{... | collective-permute-start | bytes 196616 | tf_op jit(solution)/shard_map/ppermute | solution.py:14
  127.3 1.2 copy-start.21
  127.3 1.2 copy-start.23
  134.7 0.9 copy-start.16
  135.8 34.1 %collective-permute-start.2 = (bf16[2,32,512]{2,1,0:T(8,128)(2,1)}, bf16[2,32,512]{2,1,0:T(8,128)(2,1)}, u32[]{:S(2)}, u32[]{:S(2)}) collective-permute-start(bf16[2,32,512]{2,1,0:T(8,128)(2,1)} %slice.778), channel_id=1, source_target_pairs={{1,0},{2,1},{3,2},{5,4},{6,5},{7,6},{9,8},{10,9},{11,10},{13,12},{... | collective-permute-start | bytes 196616 | tf_op jit(solution)/shard_map/ppermute | solution.py:14
  138.9 8.6 %all-to-all-start.6 = ((bf16[128,8,32]{0,2,1:T(8,128)(2,1)}), bf16[128,8,32]{0,2,1:T(8,128)(2,1)S(1)}, u32[]{:S(2)}, u32[]{:S(2)}) async-start(bf16[128,8,32]{0,2,1:T(8,128)(2,1)} %bitcast.85), calls=%async_computation.6 | async-start | bytes 131072 | tf_op jit(solution)/shard_map/all_to_all | solution.py:72
  143.1 1.6 copy-start.26
  143.1 1.6 copy-start.34
  156.0 14.8 %slice-start = ((f32[4,32,512]{2,1,0:T(8,128)}), f32[2,32,512]{2,1,0:T(8,128)S(1)}, s32[]{:S(2)}) async-start(f32[4,32,512]{2,1,0:T(8,128)} %copy-done.10), calls=%async_computation.17 | async-start | bytes 262144 | tf_op jit(solution)/shard_map/slice | solution.py:183
  156.0 14.8 %copy-start.17 = (bf16[4,32,512]{2,1,0:T(8,128)(2,1)S(1)}, bf16[4,32,512]{2,1,0:T(8,128)(2,1)}, u32[]{:S(2)}) copy-start(bf16[4,32,512]{2,1,0:T(8,128)(2,1)} %copy-done.15) | copy-start | bytes 393220
  156.0 24.8 %all-to-all-start.7 = ((bf16[128,8,32]{0,2,1:T(8,128)(2,1)}), bf16[128,8,32]{0,2,1:T(8,128)(2,1)}, u32[]{:S(2)}, u32[]{:S(2)}) async-start(bf16[128,8,32]{0,2,1:T(8,128)(2,1)} %bitcast.93), calls=%async_computation.7 | async-start | bytes 131072 | tf_op jit(solution)/shard_map/all_to_all | solution.py:72
  180.9 11.8 %all-to-all-start.14 = ((bf16[128,8,32]{0,2,1:T(8,128)(2,1)}), bf16[128,8,32]{0,2,1:T(8,128)(2,1)S(1)}, u32[]{:S(2)}, u32[]{:S(2)}) async-start(bf16[128,8,32]{0,2,1:T(8,128)(2,1)} %bitcast.166), calls=%async_computation.14 | async-start | bytes 131072 | tf_op jit(solution)/shard_map/all_to_all | solution.py:64
  185.6 0.9 copy-start.7
  186.5 0.9 copy-start.5
  189.2 1.0 copy-start.3
  192.7 9.2 %all-to-all-start.12 = ((bf16[128,8,32]{0,2,1:T(8,128)(2,1)}), bf16[128,8,32]{0,2,1:T(8,128)(2,1)S(1)}, u32[]{:S(2)}, u32[]{:S(2)}) async-start(bf16[128,8,32]{0,2,1:T(8,128)(2,1)} %bitcast.150), calls=%async_computation.12 | async-start | bytes 131072 | tf_op jit(solution)/shard_map/all_to_all | solution.py:72
  211.4 8.5 %all-to-all-start.4 = ((bf16[128,8,32]{0,2,1:T(8,128)(2,1)}), bf16[128,8,32]{0,2,1:T(8,128)(2,1)S(1)}, u32[]{:S(2)}, u32[]{:S(2)}) async-start(bf16[128,8,32]{0,2,1:T(8,128)(2,1)} %bitcast.63), calls=%async_computation.4 | async-start | bytes 131072 | tf_op jit(solution)/shard_map/all_to_all | solution.py:64
  215.6 0.9 copy-start.6
  217.3 1.0 copy-start.8
  219.9 9.1 %all-to-all-start.15 = ((bf16[128,8,32]{0,2,1:T(8,128)(2,1)}), bf16[128,8,32]{0,2,1:T(8,128)(2,1)S(1)}, u32[]{:S(2)}, u32[]{:S(2)}) async-start(bf16[128,8,32]{0,2,1:T(8,128)(2,1)} %bitcast.175), calls=%async_computation.15 | async-start | bytes 131072 | tf_op jit(solution)/shard_map/all_to_all | solution.py:64
  229.0 8.3 %all-to-all-start.13 = ((bf16[128,8,32]{0,2,1:T(8,128)(2,1)}), bf16[128,8,32]{0,2,1:T(8,128)(2,1)S(1)}, u32[]{:S(2)}, u32[]{:S(2)}) async-start(bf16[128,8,32]{0,2,1:T(8,128)(2,1)} %bitcast.155), calls=%async_computation.13 | async-start | bytes 131072 | tf_op jit(solution)/shard_map/all_to_all | solution.py:72
  242.1 1.0 copy-start.22
  245.4 1.2 copy-start.62
  245.4 1.1 copy-start.66
  245.5 7.2 %copy-start.32 = (f32[5,32,32]{2,1,0:T(8,128)S(1)}, f32[5,32,32]{2,1,0:T(8,128)}, u32[]{:S(2)}) copy-start(f32[5,32,32]{2,1,0:T(8,128)} %fusion.42) | copy-start | bytes 61444
  247.4 5.4 %copy-start.4 = (f32[4,512,32]{1,2,0:T(8,128)S(1)}, f32[4,512,32]{1,2,0:T(8,128)}, u32[]{:S(2)}) copy-start(f32[4,512,32]{1,2,0:T(8,128)} %convolution_add_fusion.6) | copy-start | bytes 786436
  247.4 11.4 %all-to-all-start.5 = ((bf16[128,8,32]{0,2,1:T(8,128)(2,1)}), bf16[128,8,32]{0,2,1:T(8,128)(2,1)S(1)}, u32[]{:S(2)}, u32[]{:S(2)}) async-start(bf16[128,8,32]{0,2,1:T(8,128)(2,1)} %bitcast.75), calls=%async_computation.5 | async-start | bytes 131072 | tf_op jit(solution)/shard_map/all_to_all | solution.py:64
  251.3 138.4 %all-reduce.3.cloned.1.call-start = ((), (), s32[]{:S(2)}) async-start(), calls=%async_computation.16 | async-start | bytes 458752 | tf_op jit(solution)/shard_map/psum | solution.py:193
  251.3 6.6 %collective-permute-start.3 = (bf16[1,32,512]{2,1,0:T(8,128)(2,1)S(1)}, bf16[1,32,512]{2,1,0:T(8,128)(2,1)S(1)}, u32[]{:S(2)}, u32[]{:S(2)}) collective-permute-start(bf16[1,32,512]{2,1,0:T(8,128)(2,1)S(1)} %slice.785), channel_id=1, source_target_pairs={{1,0},{2,1},{3,2},{5,4},{6,5},{7,6},{9,8},{10,9},{11,10},{13,12},{... | collective-permute-start | bytes 98312 | tf_op jit(solution)/shard_map/ppermute | solution.py:14
  252.8 0.9 copy-start.19
  252.8 0.9 copy-start.54
  389.7 1.6 copy-start.35
  (31 other events, 21.5 us)
Sparse Core Ops, SparseCore 0:
  264.5 125.1 all-reduce.2
where the time goes:
time: 407 us; the launch traced here: 399 us
  waiting for transfers between devices  147 us (36%)
  starting transfers between devices  83.2 us (20%)
  local copies, waits for them, and re-layouts  62.7 us (15%)
  other arithmetic  49.4 us (12%)
  matrix products  40.9 us (10%)
  between operations  16.2 us (4%)
    psum x1, waiting for transfers between devices, per_device(): conv_all, mix_all = lax.psum((conv_all, mix_all), ('graph', 'tm'))  124 us
    all_to_all x8, starting transfers between devices, push_hop(): lax.all_to_all(outgoing, 'graph', split_axis=1, concat_axis=1, tiled=True)  41.1 us
    all_to_all x8, starting transfers between devices, pull_hop(): lax.all_to_all(gather_rows(signal, tables), 'graph', split_axis=1, concat...  32.4 us
    scatter-add x24, other arithmetic, start_push(): totals = totals.at[:, columns[:, tile_slot]].add(contrib)  18.9 us
    gather x24, local copies, waits for them, and re-layouts, apply_tiles(): picked = jnp.take(blocks, columns[:, tile_slot], axis=1)  18.9 us
    scatter-add x8, other arithmetic, finish_push(): local_part.at[:, indices]  18.4 us
    unnamed x146, local copies, waits for them, and re-layouts  18.3 us
    all_to_all x8, waiting for transfers between devices, pull_hop(): lax.all_to_all(gather_rows(signal, tables), 'graph', split_axis=1, concat...  13.9 us
  transfers between devices with their start and end apart: 21, of which 9 were waited for; matrix products, arithmetic and copies ran while one was open for 23% of the time, Pallas kernels for 0%

commit v1 on v0

v1 whole, which is shorter than its diff:
```python
import functools
import math

import jax
import jax.numpy as jnp
from jax import lax
from jax.experimental import pallas as pl
from jax.experimental.pallas import tpu as pltpu
from jax.sharding import PartitionSpec as P

GATED_LAYERS = 2
HOPS = 5
BF = jnp.bfloat16
F32 = jnp.float32
MESH = pl.DeviceIdType.MESH


def dot(a, b):
    return lax.dot_general(a, b, (((1,), (0,)), ((), ())), preferred_element_type=F32)


def dot_nt(a, b):
    return lax.dot_general(a, b, (((1,), (1,)), ((), ())), preferred_element_type=F32)


def dot_tn(a, b):
    return lax.dot_general(a, b, (((0,), (0,)), ((), ())), preferred_element_type=F32)


def peers(count, body):
    if count <= 8:
        for off in range(1, count):
            body(off)
    elif count > 1:
        lax.fori_loop(1, count, lambda off, c: (body(off), c)[1], 0)


def kernel(
    n_graph, n_tm, steps, scale,
    series, cw, cb, mw, mb, tv, tcol, sidx, smask, cot,
    out, gser, gconv, gmix,
    wl, wlt, wh, wht, gm, gmt, band, mixall, ext, hops, filt, gate, flow, ctr,
    prev0, pack_s, pack_r, send, recv, e_buf, et_buf, l_buf, lt_buf,
    r_ssem, r_rsem, t_ssem, t_rsem, e_ssem, e_rsem, et_ssem, et_rsem,
    l_ssem, l_rsem, lt_ssem, lt_rsem,
):
    me = lax.axis_index("graph")
    z = lax.axis_index("tm")
    tc, sensors = series.shape
    ch = tc // steps
    half_s = sensors // 2
    slots = sidx.shape[1]
    halo = n_graph * slots
    tile = tv.shape[-1]
    rblocks, tslots = tcol.shape
    lblocks = sensors // tile
    hblocks = halo // tile
    wire = send.dtype

    barrier = pltpu.get_barrier_semaphore()

    def greet_graph(off):
        pl.semaphore_signal(barrier, inc=1, device_id={"graph": lax.rem(me + off, n_graph)}, device_id_type=MESH)

    def greet_tm(off):
        pl.semaphore_signal(barrier, inc=1, device_id={"tm": lax.rem(z + off, n_tm)}, device_id_type=MESH)

    peers(n_graph, greet_graph)
    peers(n_tm, greet_tm)
    pl.semaphore_wait(barrier, n_graph - 1 + n_tm - 1)

    def shift_copy(slot, src, dst, by):
        return pltpu.make_async_remote_copy(
            src_ref=src, dst_ref=dst, send_sem=t_ssem.at[slot], recv_sem=t_rsem.at[slot],
            device_id={"tm": lax.rem(z + by + n_tm, n_tm)}, device_id_type=MESH,
        )

    up = z < n_tm - 1
    down = z > 0

    first = shift_copy(0, series.at[pl.ds(tc - ch, ch)], prev0.at[pl.ds(tc - ch, ch)], 1)
    prev0[pl.ds(0, tc - ch), :] = jnp.zeros((tc - ch, sensors), BF)

    @pl.when(up)
    def _():
        first.start()

    row32 = lax.broadcasted_iota(jnp.int32, (ch, tc), 0)
    lane32 = lax.broadcasted_iota(jnp.int32, (ch, tc), 1)
    spread = jnp.where(lax.rem(lane32, ch) == row32, 1.0, 0.0)
    spread_b = spread.astype(BF)
    rt = lax.broadcasted_iota(jnp.int32, (tc, tc), 0) // ch
    lt = lax.broadcasted_iota(jnp.int32, (tc, tc), 1) // ch
    same = rt == lt

    def before(d):
        return lt == rt - d

    def before_prev(d):
        return lt == rt - d + steps

    cwr = dot(cw[...], spread_b)
    mwr = dot(mw[...], spread_b)

    def stack(x, base):
        return jnp.concatenate([x[base:base + ch]] * steps, axis=0)

    for l in range(GATED_LAYERS):
        d = l + 1
        for h in range(2):
            w0 = stack(cwr, (l * 2 + 0) * 2 * ch + h * ch)
            w1 = stack(cwr, (l * 2 + 1) * 2 * ch + h * ch)
            own = jnp.where(same, w0, 0.0) + jnp.where(before(d), w1, 0.0)
            band[l, pl.ds(h * tc, tc), pl.ds(0, tc)] = own.astype(BF)
            band[l, pl.ds(h * tc, tc), pl.ds(tc, tc)] = jnp.where(before_prev(d), w1, 0.0).astype(BF)
        for k in range(HOPS):
            mk = stack(mwr, (l * HOPS + k) * ch)
            mixall[l, :, pl.ds(k * tc, tc)] = jnp.where(same, mk, 0.0).astype(BF)

    r64 = lax.broadcasted_iota(jnp.int32, (2 * ch, 2 * tc), 0)
    l64 = lax.broadcasted_iota(jnp.int32, (2 * ch, 2 * tc), 1)
    spread2 = jnp.where(lax.rem(l64, ch) + (l64 // tc) * ch == r64, 1.0, 0.0)
    cbias = lax.dot_general(cb[...], spread2, (((1,), (0,)), ((), ())), precision=lax.Precision.HIGHEST, preferred_element_type=F32)
    mbias = lax.dot_general(mb[...], spread, (((1,), (0,)), ((), ())), precision=lax.Precision.HIGHEST, preferred_element_type=F32)

    for r in range(rblocks):
        tiles = [tv[r * tslots + k].astype(F32) for k in range(tslots)]
        flips = [t.T for t in tiles]
        for c in range(lblocks + hblocks):
            a = jnp.zeros((tile, tile), F32)
            b = jnp.zeros((tile, tile), F32)
            for k in range(tslots):
                on = (tcol[r, k] == c).astype(jnp.int32).astype(F32)
                a = a + tiles[k] * on
                b = b + flips[k] * on
            a = a.astype(BF)
            b = b.astype(BF)
            if c < lblocks:
                wl[pl.ds(r * tile, tile), pl.ds(c * tile, tile)] = a
                wlt[pl.ds(c * tile, tile), pl.ds(r * tile, tile)] = b
            else:
                ch_at = c - lblocks
                wh[pl.ds(r * tile, tile), pl.ds(ch_at * tile, tile)] = a
                wht[pl.ds(ch_at * tile, tile), pl.ds(r * tile, tile)] = b

    key = jnp.where(smask[...] != 0, sidx[...] + 1, 0)
    es = lax.broadcasted_iota(jnp.int32, (slots, halo), 0)
    ej = lax.broadcasted_iota(jnp.int32, (slots, halo), 1)
    pick = jnp.where(lax.rem(ej, slots) == es, 1.0, 0.0).astype(BF)
    hi = dot((key // 32).astype(F32).astype(BF), pick)
    lo = dot(lax.rem(key, 32).astype(F32).astype(BF), pick)
    pr = lax.broadcasted_iota(jnp.int32, (n_graph, halo), 0)
    pj = lax.broadcasted_iota(jnp.int32, (n_graph, halo), 1) // slots
    keys = jnp.sum(jnp.where(pr == pj, hi * 32.0 + lo, 0.0), axis=0, keepdims=True)
    ids = lax.broadcasted_iota(jnp.int32, (sensors, halo), 0).astype(F32) + 1.0
    onehot = jnp.where(ids == keys, 1.0, 0.0)
    gm[...] = onehot.astype(BF)
    gmt[...] = onehot.T.astype(BF)

    ext[0, :, pl.ds(0, tc)] = series[...].astype(F32).T.astype(BF)
    ctr[...] = cot[...].astype(F32).T

    def graph_copy(src, dst, ssem, rsem, p):
        return pltpu.make_async_remote_copy(
            src_ref=src, dst_ref=dst, send_sem=ssem, recv_sem=rsem,
            device_id={"graph": p}, device_id_type=MESH,
        )

    def tm_copy(src, dst, ssem, rsem, p):
        return pltpu.make_async_remote_copy(
            src_ref=src, dst_ref=dst, send_sem=ssem, recv_sem=rsem,
            device_id={"tm": p}, device_id_type=MESH,
        )

    def pair(r, pull_in, push_in, filler):
        sp = dot(gmt[...], pull_in)
        sb = dot(wht[...], push_in).astype(BF).astype(F32)
        send[r, :, 0] = sp.reshape(n_graph, slots, tc).astype(wire)
        send[r, :, 1] = sb.reshape(n_graph, slots, tc).astype(wire)

        def go(off):
            p = lax.rem(me + off, n_graph)
            graph_copy(send.at[r, p], recv.at[r, me], r_ssem.at[r, p], r_rsem.at[r, me], p).start()

        peers(n_graph, go)
        recv[r, me] = send[r, me]
        pulled = dot(wl[...], pull_in)
        pushed = dot(wlt[...], push_in)
        filler()

        def take(off):
            p = lax.rem(me + off, n_graph)
            graph_copy(send.at[r, p], recv.at[r, p], r_ssem.at[r, p], r_rsem.at[r, p], p).wait_recv()

        peers(n_graph, take)
        rp = recv[r, :, 0].astype(F32).reshape(halo, tc).astype(BF)
        rb = recv[r, :, 1].astype(F32).reshape(halo, tc).astype(BF)
        return pulled + dot(wh[...], rp), pushed + dot(gm[...], rb)

    lane_half = lax.broadcasted_iota(jnp.int32, (half_s, tc), 1) < tc // 2

    def pack(x):
        return jnp.where(lane_half, pltpu.roll(x[:half_s], tc // 2, 1), x[half_s:]).astype(BF)

    def unpack(p):
        x = p.astype(F32)
        return jnp.concatenate([pltpu.roll(x, tc // 2, 1), x], axis=0)

    nothing = lambda: None

    for l in range(GATED_LAYERS):
        if l == 0:
            @pl.when(down)
            def _():
                first.wait_recv()

            @pl.when(jnp.logical_not(down))
            def _():
                prev0[pl.ds(tc - ch, ch), :] = jnp.zeros((ch, sensors), BF)

            ext[0, :, pl.ds(tc, tc)] = prev0[...].astype(F32).T.astype(BF)
            pre = dot_nt(ext[0], band[0])
        else:
            pre_own = dot_nt(ext[l, :, pl.ds(0, tc)], band[l, :, pl.ds(0, tc)])

            @pl.when(down)
            def _():
                shift_copy(1, pack_s.at[0], pack_r.at[0], 1).wait_recv()

            @pl.when(jnp.logical_not(down))
            def _():
                pack_r[0] = jnp.zeros((half_s, tc), BF)

            ext[l, :, pl.ds(tc, tc)] = unpack(pack_r[0]).astype(BF)
            pre = pre_own + dot_nt(ext[l, :, pl.ds(tc, tc)], band[l, :, pl.ds(tc, tc)])
        pre = pre + cbias[l:l + 1]
        f = jnp.tanh(pre[:, :tc])
        g = jax.nn.sigmoid(pre[:, tc:])
        filt[l] = f
        gate[l] = g
        gated = (f * g).astype(BF)
        hops[l, :, pl.ds(0, tc)] = gated
        fo, bo = pair(2 * l, gated, gated, nothing)
        fo = fo.astype(BF)
        bo = bo.astype(BF)
        hops[l, :, pl.ds(tc, tc)] = fo
        hops[l, :, pl.ds(3 * tc, tc)] = bo
        part = []

        def mix_early():
            m = dot_nt(hops[l, :, pl.ds(0, 2 * tc)], mixall[l, :, pl.ds(0, 2 * tc)])
            part.append(m + dot_nt(hops[l, :, pl.ds(3 * tc, tc)], mixall[l, :, pl.ds(3 * tc, tc)]))

        f2, b2 = pair(2 * l + 1, fo, bo, mix_early)
        f2 = f2.astype(BF)
        b2 = b2.astype(BF)
        hops[l, :, pl.ds(2 * tc, tc)] = f2
        hops[l, :, pl.ds(4 * tc, tc)] = b2
        mixed = part[0] + dot_nt(f2, mixall[l, :, pl.ds(2 * tc, tc)]) + dot_nt(b2, mixall[l, :, pl.ds(4 * tc, tc)])
        mixed = mixed + mbias[l:l + 1]
        hid = ext[l, :, pl.ds(0, tc)].astype(F32) + mixed
        if l + 1 < GATED_LAYERS:
            pack_s[0] = pack(hid)

            @pl.when(up)
            def _():
                shift_copy(1, pack_s.at[0], pack_r.at[0], 1).start()

            ext[l + 1, :, pl.ds(0, tc)] = hid.astype(BF)
        else:
            out[...] = hid.T.astype(BF)

    flow[...] = ctr[...]

    lane_g = lax.broadcasted_iota(jnp.int32, (ch, tc), 1) // ch

    def fold(x):
        y = x[0:ch]
        for t in range(1, steps):
            y = y + x[t * ch:(t + 1) * ch]
        sh = ch
        while sh < tc:
            y = y + pltpu.roll(y, sh, 1)
            sh *= 2
        return y

    def lanes_of(xs):
        y = jnp.zeros((ch, tc), F32)
        for g, x in enumerate(xs):
            y = jnp.where(lane_g == g, x, y)
        return y

    e_conv = None
    e_mix = [None, None]

    def gather_start(buf, ssem, rsem, count, here, copy):
        def go(off):
            p = lax.rem(here + off, count)
            copy(buf.at[here], buf.at[here], ssem.at[p], rsem.at[here], p).start()

        peers(count, go)

    def gather_sum(buf, ssem, rsem, count, here, copy):
        def take(off):
            p = lax.rem(here + off, count)
            copy(buf.at[p], buf.at[p], ssem.at[p], rsem.at[p], p).wait_recv()

        peers(count, take)
        total = buf[0]
        for p in range(1, count):
            total = total + buf[p]
        return total

    for l in reversed(range(GATED_LAYERS)):
        d = l + 1
        fr = flow[...].astype(BF)
        r0 = 2 * GATED_LAYERS + 2 * (GATED_LAYERS - 1 - l)

        def back(k):
            return dot(fr, mixall[l, :, pl.ds(k * tc, tc)])

        rest = []

        def fill_one():
            rest.extend([back(0), back(1), back(3)])
            prod = dot_tn(fr, hops[l])
            folds = [fold(jnp.where(same, prod[:, k * tc:(k + 1) * tc], 0.0)) for k in range(HOPS)]
            e_mix[l] = (lanes_of(folds[:4]), folds[4])
            if l == 0:
                e_buf[me] = jnp.concatenate(
                    [e_conv, e_mix[1][0], e_mix[0][0], lanes_of([e_mix[1][1], e_mix[0][1]])], axis=0
                )
                gather_start(e_buf, e_ssem, e_rsem, n_graph, me, graph_copy)

        bi, fi = pair(r0, back(4).astype(BF), back(2).astype(BF), fill_one)

        def fill_two():
            if l == 0:
                et_buf[z] = gather_sum(e_buf, e_ssem, e_rsem, n_graph, me, graph_copy)
                gather_start(et_buf, et_ssem, et_rsem, n_tm, z, tm_copy)

        bo, fo = pair(r0 + 1, (rest[2] + bi).astype(BF), (rest[1] + fi).astype(BF), fill_two)
        gg = rest[0] + fo + bo
        f = filt[l]
        g = gate[l]
        gf = gg * g * (1.0 - f * f)
        gt = gg * f * g * (1.0 - g)
        gp = jnp.concatenate([gf, gt], axis=1).astype(BF)
        slot = 2 + (GATED_LAYERS - 1 - l)
        at = 1 + (GATED_LAYERS - 1 - l)
        pack_s[at] = pack(dot(gp, band[l, :, pl.ds(tc, tc)]))

        @pl.when(down)
        def _():
            shift_copy(slot, pack_s.at[at], pack_r.at[at], -1).start()

        prod = dot_tn(gp, ext[l])
        pieces = []
        for tap in range(2):
            for h in range(2):
                own = prod[h * tc:(h + 1) * tc, :tc]
                if tap == 0:
                    x = jnp.where(same, own, 0.0)
                else:
                    x = jnp.where(before(d), own, 0.0) + jnp.where(before_prev(d), prod[h * tc:(h + 1) * tc, tc:], 0.0)
                pieces.append(fold(x))
        conv = lanes_of(pieces)
        if l == 0:
            l_buf[me] = conv
            gather_start(l_buf, l_ssem, l_rsem, n_graph, me, graph_copy)
        else:
            e_conv = conv
        new = flow[...] + dot(gp, band[l, :, pl.ds(0, tc)])

        @pl.when(up)
        def _():
            shift_copy(slot, pack_s.at[at], pack_r.at[at], -1).wait_recv()

        @pl.when(jnp.logical_not(up))
        def _():
            pack_r[at] = jnp.zeros((half_s, tc), BF)

        lanes = lax.broadcasted_iota(jnp.int32, (sensors, tc), 1)
        flow[...] = new + jnp.where(lanes >= tc // 2, unpack(pack_r[at]), 0.0)

    lt_buf[z] = gather_sum(l_buf, l_ssem, l_rsem, n_graph, me, graph_copy)
    gather_start(lt_buf, lt_ssem, lt_rsem, n_tm, z, tm_copy)
    gser[...] = flow[...].T.astype(BF)

    def lane_group(x, g):
        return (pltpu.roll(x, tc - g * ch, 1) if g else x)[:, :ch]

    def put_conv(l, x):
        for tap in range(2):
            for h in range(2):
                gconv[l, tap, pl.ds(h * ch, ch), :] = lane_group(x, tap * 2 + h)

    e = gather_sum(et_buf, et_ssem, et_rsem, n_tm, z, tm_copy) * scale
    put_conv(1, e[:ch])
    for k in range(4):
        gmix[1, k] = lane_group(e[ch:2 * ch], k)
        gmix[0, k] = lane_group(e[2 * ch:3 * ch], k)
    gmix[1, 4] = lane_group(e[3 * ch:], 0)
    gmix[0, 4] = lane_group(e[3 * ch:], 1)
    put_conv(0, gather_sum(lt_buf, lt_ssem, lt_rsem, n_tm, z, tm_copy) * scale)

    def sent_graph(off):
        p = lax.rem(me + off, n_graph)
        for r in range(4 * GATED_LAYERS):
            graph_copy(send.at[r, p], recv.at[r, me], r_ssem.at[r, p], r_rsem.at[r, me], p).wait_send()
        graph_copy(e_buf.at[me], e_buf.at[me], e_ssem.at[p], e_rsem.at[me], p).wait_send()
        graph_copy(l_buf.at[me], l_buf.at[me], l_ssem.at[p], l_rsem.at[me], p).wait_send()

    peers(n_graph, sent_graph)

    def sent_tm(off):
        p = lax.rem(z + off, n_tm)
        tm_copy(et_buf.at[z], et_buf.at[z], et_ssem.at[p], et_rsem.at[z], p).wait_send()
        tm_copy(lt_buf.at[z], lt_buf.at[z], lt_ssem.at[p], lt_rsem.at[z], p).wait_send()

    peers(n_tm, sent_tm)

    @pl.when(up)
    def _():
        first.wait_send()
        shift_copy(1, pack_s.at[0], pack_r.at[0], 1).wait_send()

    @pl.when(down)
    def _():
        shift_copy(2, pack_s.at[1], pack_r.at[1], -1).wait_send()
        shift_copy(3, pack_s.at[2], pack_r.at[2], -1).wait_send()


def per_device(series, cw, cb, mw, mb, tv, tcol, sidx, smask, cot):
    n_graph = lax.axis_size("graph")
    n_tm = lax.axis_size("tm")
    steps, ch, sensors = series.shape
    tc = steps * ch
    slots = sidx.shape[2]
    halo = n_graph * slots
    wire = BF if slots % 16 == 0 else F32
    rounds = 4 * GATED_LAYERS
    scale = 1.0 / math.sqrt(float(steps * n_tm * sensors * n_graph))
    vm = pl.BlockSpec(memory_space=pltpu.VMEM)
    sm = pl.BlockSpec(memory_space=pltpu.SMEM)
    dma = pltpu.SemaphoreType.DMA
    out, gser, gconv, gmix = pl.pallas_call(
        functools.partial(kernel, n_graph, n_tm, steps, scale),
        out_shape=(
            jax.ShapeDtypeStruct((tc, sensors), BF),
            jax.ShapeDtypeStruct((tc, sensors), BF),
            jax.ShapeDtypeStruct(cw.shape, F32),
            jax.ShapeDtypeStruct(mw.shape, F32),
        ),
        in_specs=[vm] * 6 + [sm] + [vm] * 3,
        out_specs=(vm,) * 4,
        scratch_shapes=[
            pltpu.VMEM((sensors, sensors), BF),
            pltpu.VMEM((sensors, sensors), BF),
            pltpu.VMEM((sensors, halo), BF),
            pltpu.VMEM((halo, sensors), BF),
            pltpu.VMEM((sensors, halo), BF),
            pltpu.VMEM((halo, sensors), BF),
            pltpu.VMEM((GATED_LAYERS, 2 * tc, 2 * tc), BF),
            pltpu.VMEM((GATED_LAYERS, tc, HOPS * tc), BF),
            pltpu.VMEM((GATED_LAYERS, sensors, 2 * tc), BF),
            pltpu.VMEM((GATED_LAYERS, sensors, HOPS * tc), BF),
            pltpu.VMEM((GATED_LAYERS, sensors, tc), F32),
            pltpu.VMEM((GATED_LAYERS, sensors, tc), F32),
            pltpu.VMEM((sensors, tc), F32),
            pltpu.VMEM((sensors, tc), F32),
            pltpu.VMEM((tc, sensors), BF),
            pltpu.VMEM((3, sensors // 2, tc), BF),
            pltpu.VMEM((3, sensors // 2, tc), BF),
            pltpu.VMEM((rounds, n_graph, 2, slots, tc), wire),
            pltpu.VMEM((rounds, n_graph, 2, slots, tc), wire),
            pltpu.VMEM((n_graph, 4 * ch, tc), F32),
            pltpu.VMEM((n_tm, 4 * ch, tc), F32),
            pltpu.VMEM((n_graph, ch, tc), F32),
            pltpu.VMEM((n_tm, ch, tc), F32),
            dma((rounds, n_graph)), dma((rounds, n_graph)),
            dma((4,)), dma((4,)),
            dma((n_graph,)), dma((n_graph,)),
            dma((n_tm,)), dma((n_tm,)),
            dma((n_graph,)), dma((n_graph,)),
            dma((n_tm,)), dma((n_tm,)),
        ],
        compiler_params=pltpu.CompilerParams(
            collective_id=0, has_side_effects=True, vmem_limit_bytes=48 * 1024 * 1024
        ),
    )(
        series.reshape(tc, sensors),
        cw.reshape(-1, ch),
        cb,
        mw.reshape(-1, ch),
        mb,
        tv.reshape(-1, *tv.shape[2:]),
        tcol,
        sidx[0],
        smask[0],
        cot.reshape(tc, sensors),
    )
    return out.reshape(series.shape), gser.reshape(series.shape), gconv, gmix


def solution(mesh):
    return jax.shard_map(
        per_device,
        mesh=mesh,
        in_specs=(
            P("tm", None, "graph"),
            P(),
            P(),
            P(),
            P(),
            P("graph", None, None, None),
            P("graph", None),
            P("graph", None, None),
            P("graph", None, None),
            P("tm", None, "graph"),
        ),
        out_specs=(P("tm", None, "graph"), P("tm", None, "graph"), P(), P()),
        check_vma=False,
    )
```

time: 407 us -> 72.4 us (0.18); the launches traced: 399 us -> 72.2 us
  waiting for transfers between devices: 147 us -> 0 us
  starting transfers between devices: 83.2 us -> 0 us
  Pallas kernels: 0 us -> 64.4 us
  local copies, waits for them, and re-layouts: 62.7 us -> 7.05 us
  other arithmetic: 49.4 us -> 0 us
  matrix products: 40.9 us -> 0 us
  between operations: 16.2 us -> 0.73 us
    psum x1 -> x0, waiting for transfers between devices: 124 us -> none  [per_device(): conv_all, mix_all = lax.psum((conv_all, mix_all), ('graph', 'tm'))]
    all_to_all x16 -> x0, starting transfers between devices: 73.5 us -> none  [the longest x8 41.1 us: push_hop(): lax.all_to_all(outgoing, 'graph', split_axis=1, concat_axis=1, tiled=True)]
    pallas_call x0 -> x1, Pallas kernels: none -> 64.4 us  [per_device(): pl.pallas_call(functools.partial(kernel, n_graph, n_tm, steps, scale), ou...]
    dot_general x90 -> x0, matrix products: 40.9 us -> none  [the longest x14 10.9 us: channel_back(): jnp.einsum('oc,ton->tcn', matrix, signal, preferred_element_type=jnp.floa...]
    scatter-add x32 -> x0, other arithmetic: 37.3 us -> none  [the longest x24 18.9 us: start_push(): totals = totals.at[:, columns[:, tile_slot]].add(contrib)]
    gather x32 -> x0, local copies, waits for them, and re-layouts: 27.6 us -> none  [the longest x24 18.9 us: apply_tiles(): picked = jnp.take(blocks, columns[:, tile_slot], axis=1)]
    all_to_all x16 -> x0, waiting for transfers between devices: 19.5 us -> none  [the longest x8 13.9 us: pull_hop(): lax.all_to_all(gather_rows(signal, tables), 'graph', split_axis=1, concat...]
    unnamed x146 -> x23, local copies, waits for them, and re-layouts: 18.3 us -> 7.05 us
  transfers between devices with their start and end apart: 21 -> 0, of which waited for: 9 -> 0; matrix products, arithmetic and copies ran while one was open for 23% -> 0% of each run, Pallas kernels for 0% -> 0%
where the time goes in v1:
time: 72.4 us; the launch traced here: 72.2 us
  Pallas kernels  64.4 us (89%)
  local copies, waits for them, and re-layouts  7.05 us (10%)
  between operations  0.73 us (1%)
    pallas_call x1, Pallas kernels, per_device(): pl.pallas_call(functools.partial(kernel, n_graph, n_tm, steps, scale), ou...  64.4 us
    unnamed x23, local copies, waits for them, and re-layouts  7.05 us

profile of v1, /device:TPU:0, one launch (start us, length us, event | category | flops | bytes accessed | tf_op | source)
XLA Modules:
  0.0 72.2 jit_solution(17911044709337977877)
XLA Ops:
  0.6 0.0 copy-start.3
  0.6 0.0 copy-start.4
  0.7 0.0 copy-start.5
  0.7 0.0 copy-start.6
  0.7 0.0 copy-start.8
  0.7 0.9 %copy.14 = bf16[2,2,64,32]{3,2,1,0:T(8,128)(2,1)S(1)} copy(bf16[2,2,64,32]{2,3,1,0:T(8,128)(2,1)} %param.11) | data formatting | bytes 32768 | tf_op args[1]
  1.6 0.0 copy-start.7
  1.6 0.0 copy-done.3
  1.6 0.0 copy-done.4
  1.6 0.0 copy-done.5
  1.6 0.0 copy-done.6
  1.6 0.0 copy-done.8
  1.7 0.6 copy-done.7
  2.3 0.0 copy-start
  2.3 1.0 %copy-done = bf16[4,3,128,128]{3,2,1,0:T(8,128)(2,1)S(1)} copy-done((bf16[4,3,128,128]{3,2,1,0:T(8,128)(2,1)S(1)}, bf16[4,3,128,128]{3,2,1,0:T(8,128)(2,1)}, u32[]{:S(2)}) %copy-start) | copy-done | bytes 393240
  3.3 0.0 copy-start.1
  3.3 0.9 %copy-done.1 = bf16[4,32,512]{2,1,0:T(8,128)(2,1)S(1)} copy-done((bf16[4,32,512]{2,1,0:T(8,128)(2,1)S(1)}, bf16[4,32,512]{2,1,0:T(8,128)(2,1)}, u32[]{:S(2)}) %copy-start.1) | copy-done | bytes 131096
  4.2 0.0 copy-start.2
  4.2 0.9 %copy-done.2 = bf16[4,32,512]{2,1,0:T(8,128)(2,1)S(1)} copy-done((bf16[4,32,512]{2,1,0:T(8,128)(2,1)S(1)}, bf16[4,32,512]{2,1,0:T(8,128)(2,1)}, u32[]{:S(2)}) %copy-start.2) | copy-done | bytes 131096
  5.1 64.4 %shard_map.129 = (bf16[128,512]{1,0:T(8,128)(2,1)S(1)}, bf16[128,512]{1,0:T(8,128)(2,1)S(1)}, f32[2,2,64,32]{3,2,1,0:T(8,128)S(1)}, f32[2,5,32,32]{3,2,1,0:T(8,128)S(1)}) custom-call(bf16[128,512]{1,0:T(8,128)(2,1)S(1)} %bitcast.11, bf16[256,32]{1,0:T(8,128)(2,1)S(1)} %bitcast.10, f32[2,64]{1,0:T(2,128)S(1)} %copy-done.7, bf16[320,32]{1,0:T(8,128)(2,1)S(1)} %bitcast.15, ...), custom_call_target="tpu_custom_call" | custom-call | tf_op jit(solution)/shard_map/pallas_call | solution.py:447
  69.5 0.7 %copy.15 = f32[2,2,64,32]{2,3,1,0:T(8,128)} copy(f32[2,2,64,32]{3,2,1,0:T(8,128)S(1)} %get-tuple-element.14) | data formatting | bytes 65536
  70.2 0.7 copy.19
  70.8 0.7 copy.20
  71.5 0.7 copy.21
Async XLA Ops:
  0.6 1.0 %copy-start.3 = (bf16[2,5,32,32]{3,2,1,0:T(8,128)(2,1)S(1)}, bf16[2,5,32,32]{3,2,1,0:T(8,128)(2,1)}, u32[]{:S(2)}) copy-start(bf16[2,5,32,32]{3,2,1,0:T(8,128)(2,1)} %param.13) | copy-start | bytes 61444
  0.6 1.0 %copy-start.4 = (s32[1,8,32]{2,1,0:T(8,128)S(1)}, s32[1,8,32]{2,1,0:T(8,128)}, u32[]{:S(2)}) copy-start(s32[1,8,32]{2,1,0:T(8,128)} %param.17) | copy-start | bytes 3076
  0.7 1.0 %copy-start.5 = (s32[1,8,32]{2,1,0:T(8,128)S(1)}, s32[1,8,32]{2,1,0:T(8,128)}, u32[]{:S(2)}) copy-start(s32[1,8,32]{2,1,0:T(8,128)} %param.18) | copy-start | bytes 3076
  0.7 1.0 %copy-start.6 = (s32[4,3]{1,0:T(4,128)S(1)}, s32[4,3]{1,0:T(4,128)}, u32[]{:S(2)}) copy-start(s32[4,3]{1,0:T(4,128)} %tcol.1) | copy-start | bytes 148
  0.7 1.0 %copy-start.8 = (f32[2,32]{1,0:T(2,128)S(1)}, f32[2,32]{1,0:T(2,128)}, u32[]{:S(2)}) copy-start(f32[2,32]{1,0:T(2,128)} %mb.1) | copy-start | bytes 772
  1.6 0.7 copy-start.7
  2.3 1.0 %copy-start = (bf16[4,3,128,128]{3,2,1,0:T(8,128)(2,1)S(1)}, bf16[4,3,128,128]{3,2,1,0:T(8,128)(2,1)}, u32[]{:S(2)}) copy-start(bf16[4,3,128,128]{3,2,1,0:T(8,128)(2,1)} %param.15) | copy-start | bytes 1179652
  3.3 0.9 %copy-start.1 = (bf16[4,32,512]{2,1,0:T(8,128)(2,1)S(1)}, bf16[4,32,512]{2,1,0:T(8,128)(2,1)}, u32[]{:S(2)}) copy-start(bf16[4,32,512]{2,1,0:T(8,128)(2,1)} %param.10) | copy-start | bytes 393220
  4.2 0.9 %copy-start.2 = (bf16[4,32,512]{2,1,0:T(8,128)(2,1)S(1)}, bf16[4,32,512]{2,1,0:T(8,128)(2,1)}, u32[]{:S(2)}) copy-start(bf16[4,32,512]{2,1,0:T(8,128)(2,1)} %param.19) | copy-start | bytes 393220

commit v2 on v1

--- a/solution.py
+++ b/solution.py
@@ -37,12 +37,13 @@
 
 def kernel(
     n_graph, n_tm, steps, scale,
-    series, cw, cb, mw, mb, tv, tcol, sidx, smask, cot,
+    series_h, cw_h, cb_h, mw_h, mb_h, tv_h, tcol, sidx_h, smask_h, cot_h,
     out, gser, gconv, gmix,
-    wl, wlt, wh, wht, gm, gmt, band, mixall, ext, hops, filt, gate, flow, ctr,
+    wl, wlt, wh, wht, gm, gmt, band, mixall, ext, hops, filt, gate, flow, ctr, hid_end,
     prev0, pack_s, pack_r, send, recv, e_buf, et_buf, l_buf, lt_buf,
+    e_part, eg_buf, series, cw, cb, mw, mb, tv, sidx, smask, cot, in_sem,
     r_ssem, r_rsem, t_ssem, t_rsem, e_ssem, e_rsem, et_ssem, et_rsem,
-    l_ssem, l_rsem, lt_ssem, lt_rsem,
+    l_ssem, l_rsem, lt_ssem, lt_rsem, eg_ssem, eg_rsem,
 ):
     me = lax.axis_index("graph")
     z = lax.axis_index("tm")
@@ -56,7 +57,17 @@
     lblocks = sensors // tile
     hblocks = halo // tile
     wire = send.dtype
-
+    er = e_part.shape[1]
+
+    loads = [
+        pltpu.make_async_copy(src, dst, in_sem.at[i])
+        for i, (src, dst) in enumerate(
+            ((cw_h, cw), (mw_h, mw), (cb_h, cb), (mb_h, mb), (tv_h, tv), (series_h, series),
+             (sidx_h, sidx), (smask_h, smask), (cot_h, cot))
+        )
+    ]
+    for load in loads:
+        load.start()
     barrier = pltpu.get_barrier_semaphore()
 
     def greet_graph(off):
@@ -67,7 +78,6 @@
 
     peers(n_graph, greet_graph)
     peers(n_tm, greet_tm)
-    pl.semaphore_wait(barrier, n_graph - 1 + n_tm - 1)
 
     def shift_copy(slot, src, dst, by):
         return pltpu.make_async_remote_copy(
@@ -78,12 +88,8 @@
     up = z < n_tm - 1
     down = z > 0
 
-    first = shift_copy(0, series.at[pl.ds(tc - ch, ch)], prev0.at[pl.ds(tc - ch, ch)], 1)
+    first = shift_copy(0, series_h.at[pl.ds(tc - ch, ch)], prev0.at[pl.ds(tc - ch, ch)], 1)
     prev0[pl.ds(0, tc - ch), :] = jnp.zeros((tc - ch, sensors), BF)
-
-    @pl.when(up)
-    def _():
-        first.start()
 
     row32 = lax.broadcasted_iota(jnp.int32, (ch, tc), 0)
     lane32 = lax.broadcasted_iota(jnp.int32, (ch, tc), 1)
@@ -99,7 +105,19 @@
     def before_prev(d):
         return lt == rt - d + steps
 
-    cwr = dot(cw[...], spread_b)
+    for load in loads[:4]:
+        load.wait()
+    taps = 2 * GATED_LAYERS
+    rs = lax.broadcasted_iota(jnp.int32, (taps * ch, taps * tc), 0)
+    ls = lax.broadcasted_iota(jnp.int32, (taps * ch, taps * tc), 1)
+    spread_taps = jnp.where((ls // tc) * ch + lax.rem(ls, ch) == rs, 1.0, 0.0).astype(BF)
+    def after(d):
+        return rt == lt - d
+
+    def after_prev(d):
+        return rt == lt - d + steps
+
+    cwr = dot_tn(cw[...], spread_taps)
     mwr = dot(mw[...], spread_b)
 
     def stack(x, base):
@@ -108,8 +126,8 @@
     for l in range(GATED_LAYERS):
         d = l + 1
         for h in range(2):
-            w0 = stack(cwr, (l * 2 + 0) * 2 * ch + h * ch)
-            w1 = stack(cwr, (l * 2 + 1) * 2 * ch + h * ch)
+            w0 = stack(cwr[:, (l * 2) * tc:(l * 2 + 1) * tc], h * ch)
+            w1 = stack(cwr[:, (l * 2 + 1) * tc:(l * 2 + 2) * tc], h * ch)
             own = jnp.where(same, w0, 0.0) + jnp.where(before(d), w1, 0.0)
             band[l, pl.ds(h * tc, tc), pl.ds(0, tc)] = own.astype(BF)
             band[l, pl.ds(h * tc, tc), pl.ds(tc, tc)] = jnp.where(before_prev(d), w1, 0.0).astype(BF)
@@ -123,6 +141,14 @@
     cbias = lax.dot_general(cb[...], spread2, (((1,), (0,)), ((), ())), precision=lax.Precision.HIGHEST, preferred_element_type=F32)
     mbias = lax.dot_general(mb[...], spread, (((1,), (0,)), ((), ())), precision=lax.Precision.HIGHEST, preferred_element_type=F32)
 
+    pl.semaphore_wait(barrier, n_graph - 1 + n_tm - 1)
+
+    @pl.when(up)
+    def _():
+        first.start()
+
+    for load in loads[4:]:
+        load.wait()
     for r in range(rblocks):
         tiles = [tv[r * tslots + k].astype(F32) for k in range(tslots)]
         flips = [t.T for t in tiles]
@@ -158,7 +184,6 @@
     gmt[...] = onehot.T.astype(BF)
 
     ext[0, :, pl.ds(0, tc)] = series[...].astype(F32).T.astype(BF)
-    ctr[...] = cot[...].astype(F32).T
 
     def graph_copy(src, dst, ssem, rsem, p):
         return pltpu.make_async_remote_copy(
@@ -206,7 +231,8 @@
         x = p.astype(F32)
         return jnp.concatenate([pltpu.roll(x, tc // 2, 1), x], axis=0)
 
-    nothing = lambda: None
+    def take_cotangent():
+        ctr[...] = cot[...].astype(F32).T
 
     for l in range(GATED_LAYERS):
         if l == 0:
@@ -240,7 +266,7 @@
         gate[l] = g
         gated = (f * g).astype(BF)
         hops[l, :, pl.ds(0, tc)] = gated
-        fo, bo = pair(2 * l, gated, gated, nothing)
+        fo, bo = pair(2 * l, gated, gated, take_cotangent if l == 0 else (lambda: None))
         fo = fo.astype(BF)
         bo = bo.astype(BF)
         hops[l, :, pl.ds(tc, tc)] = fo
@@ -268,7 +294,7 @@
 
             ext[l + 1, :, pl.ds(0, tc)] = hid.astype(BF)
         else:
-            out[...] = hid.T.astype(BF)
+            hid_end[...] = hid
 
     flow[...] = ctr[...]
 
@@ -325,12 +351,22 @@
             rest.extend([back(0), back(1), back(3)])
             prod = dot_tn(fr, hops[l])
             folds = [fold(jnp.where(same, prod[:, k * tc:(k + 1) * tc], 0.0)) for k in range(HOPS)]
+            if l == GATED_LAYERS - 1:
+                out[...] = hid_end[...].T.astype(BF)
             e_mix[l] = (lanes_of(folds[:4]), folds[4])
             if l == 0:
-                e_buf[me] = jnp.concatenate(
+                early = jnp.concatenate(
                     [e_conv, e_mix[1][0], e_mix[0][0], lanes_of([e_mix[1][1], e_mix[0][1]])], axis=0
                 )
-                gather_start(e_buf, e_ssem, e_rsem, n_graph, me, graph_copy)
+                for p in range(n_graph):
+                    e_part[p] = early[p * er:(p + 1) * er]
+
+                def scatter(off):
+                    p = lax.rem(me + off, n_graph)
+                    graph_copy(e_part.at[p], e_buf.at[me], e_ssem.at[p], e_rsem.at[me], p).start()
+
+                peers(n_graph, scatter)
+                e_buf[me] = e_part[me]
 
         bi, fi = pair(r0, back(4).astype(BF), back(2).astype(BF), fill_one)
 
@@ -354,20 +390,22 @@
         def _():
             shift_copy(slot, pack_s.at[at], pack_r.at[at], -1).start()
 
-        prod = dot_tn(gp, ext[l])
+        prod = dot_tn(ext[l], gp)
         pieces = []
         for tap in range(2):
             for h in range(2):
-                own = prod[h * tc:(h + 1) * tc, :tc]
+                own = prod[:tc, h * tc:(h + 1) * tc]
                 if tap == 0:
                     x = jnp.where(same, own, 0.0)
                 else:
-                    x = jnp.where(before(d), own, 0.0) + jnp.where(before_prev(d), prod[h * tc:(h + 1) * tc, tc:], 0.0)
+                    x = jnp.where(after(d), own, 0.0) + jnp.where(after_prev(d), prod[tc:, h * tc:(h + 1) * tc], 0.0)
                 pieces.append(fold(x))
         conv = lanes_of(pieces)
         if l == 0:
             l_buf[me] = conv
             gather_start(l_buf, l_ssem, l_rsem, n_graph, me, graph_copy)
+            eg_buf[me] = gather_sum(et_buf, et_ssem, et_rsem, n_tm, z, tm_copy)
+            gather_start(eg_buf, eg_ssem, eg_rsem, n_graph, me, graph_copy)
         else:
             e_conv = conv
         new = flow[...] + dot(gp, band[l, :, pl.ds(0, tc)])
@@ -391,11 +429,15 @@
         return (pltpu.roll(x, tc - g * ch, 1) if g else x)[:, :ch]
 
     def put_conv(l, x):
-        for tap in range(2):
-            for h in range(2):
-                gconv[l, tap, pl.ds(h * ch, ch), :] = lane_group(x, tap * 2 + h)
-
-    e = gather_sum(et_buf, et_ssem, et_rsem, n_tm, z, tm_copy) * scale
+        gconv[l, 0] = x[:, :2 * ch]
+        gconv[l, 1] = pltpu.roll(x, tc - 2 * ch, 1)[:, :2 * ch]
+
+    def take_group(off):
+        p = lax.rem(me + off, n_graph)
+        graph_copy(eg_buf.at[p], eg_buf.at[p], eg_ssem.at[p], eg_rsem.at[p], p).wait_recv()
+
+    peers(n_graph, take_group)
+    e = jnp.concatenate([eg_buf[p] for p in range(n_graph)], axis=0) * scale
     put_conv(1, e[:ch])
     for k in range(4):
         gmix[1, k] = lane_group(e[ch:2 * ch], k)
@@ -408,7 +450,8 @@
         p = lax.rem(me + off, n_graph)
         for r in range(4 * GATED_LAYERS):
             graph_copy(send.at[r, p], recv.at[r, me], r_ssem.at[r, p], r_rsem.at[r, me], p).wait_send()
-        graph_copy(e_buf.at[me], e_buf.at[me], e_ssem.at[p], e_rsem.at[me], p).wait_send()
+        graph_copy(e_part.at[p], e_buf.at[me], e_ssem.at[p], e_rsem.at[me], p).wait_send()
+        graph_copy(eg_buf.at[me], eg_buf.at[me], eg_ssem.at[p], eg_rsem.at[me], p).wait_send()
         graph_copy(l_buf.at[me], l_buf.at[me], l_ssem.at[p], l_rsem.at[me], p).wait_send()
 
     peers(n_graph, sent_graph)
@@ -429,6 +472,17 @@
     def _():
         shift_copy(2, pack_s.at[1], pack_r.at[1], -1).wait_send()
         shift_copy(3, pack_s.at[2], pack_r.at[2], -1).wait_send()
+
+
+def store_kernel(a, b, c, d, ao, bo, co, do, sem):
+    copies = [
+        pltpu.make_async_copy(src, dst, sem.at[i])
+        for i, (src, dst) in enumerate(((a, ao), (b, bo), (c, co), (d, do)))
+    ]
+    for copy in copies:
+        copy.start()
+    for copy in copies:
+        copy.wait()
 
 
 def per_device(series, cw, cb, mw, mb, tv, tcol, sidx, smask, cot):
@@ -442,6 +496,21 @@
     rounds = 4 * GATED_LAYERS
     scale = 1.0 / math.sqrt(float(steps * n_tm * sensors * n_graph))
     vm = pl.BlockSpec(memory_space=pltpu.VMEM)
+    hb = pl.BlockSpec(memory_space=pltpu.HBM)
+    cwt_shape = (*cw.shape[:2], cw.shape[3], cw.shape[2])
+    ins = (
+        series.reshape(tc, sensors),
+        jnp.swapaxes(cw, 2, 3).reshape(-1, cw.shape[2]),
+        cb,
+        mw.reshape(-1, ch),
+        mb,
+        tv.reshape(-1, *tv.shape[2:]),
+        tcol,
+        sidx[0],
+        smask[0],
+        cot.reshape(tc, sensors),
+    )
+    er = 4 * ch // n_graph
     sm = pl.BlockSpec(memory_space=pltpu.SMEM)
     dma = pltpu.SemaphoreType.DMA
     out, gser, gconv, gmix = pl.pallas_call(
@@ -449,10 +518,10 @@
         out_shape=(
             jax.ShapeDtypeStruct((tc, sensors), BF),
             jax.ShapeDtypeStruct((tc, sensors), BF),
-            jax.ShapeDtypeStruct(cw.shape, F32),
+            jax.ShapeDtypeStruct(cwt_shape, F32),
             jax.ShapeDtypeStruct(mw.shape, F32),
         ),
-        in_specs=[vm] * 6 + [sm] + [vm] * 3,
+        in_specs=[hb] * 6 + [sm] + [hb] * 3,
         out_specs=(vm,) * 4,
         scratch_shapes=[
             pltpu.VMEM((sensors, sensors), BF),
@@ -469,37 +538,41 @@
             pltpu.VMEM((GATED_LAYERS, sensors, tc), F32),
             pltpu.VMEM((sensors, tc), F32),
             pltpu.VMEM((sensors, tc), F32),
+            pltpu.VMEM((sensors, tc), F32),
             pltpu.VMEM((tc, sensors), BF),
             pltpu.VMEM((3, sensors // 2, tc), BF),
             pltpu.VMEM((3, sensors // 2, tc), BF),
             pltpu.VMEM((rounds, n_graph, 2, slots, tc), wire),
             pltpu.VMEM((rounds, n_graph, 2, slots, tc), wire),
-            pltpu.VMEM((n_graph, 4 * ch, tc), F32),
-            pltpu.VMEM((n_tm, 4 * ch, tc), F32),
+            pltpu.VMEM((n_graph, er, tc), F32),
+            pltpu.VMEM((n_tm, er, tc), F32),
             pltpu.VMEM((n_graph, ch, tc), F32),
             pltpu.VMEM((n_tm, ch, tc), F32),
+            pltpu.VMEM((n_graph, er, tc), F32),
+            pltpu.VMEM((n_graph, er, tc), F32),
+            *[pltpu.VMEM(x.shape, x.dtype) for x in ins[:6] + ins[7:]],
+            dma((9,)),
             dma((rounds, n_graph)), dma((rounds, n_graph)),
             dma((4,)), dma((4,)),
             dma((n_graph,)), dma((n_graph,)),
             dma((n_tm,)), dma((n_tm,)),
             dma((n_graph,)), dma((n_graph,)),
             dma((n_tm,)), dma((n_tm,)),
+            dma((n_graph,)), dma((n_graph,)),
         ],
         compiler_params=pltpu.CompilerParams(
-            collective_id=0, has_side_effects=True, vmem_limit_bytes=48 * 1024 * 1024
+            collective_id=0, has_side_effects=True, vmem_limit_bytes=63 * 1024 * 1024
         ),
-    )(
-        series.reshape(tc, sensors),
-        cw.reshape(-1, ch),
-        cb,
-        mw.reshape(-1, ch),
-        mb,
-        tv.reshape(-1, *tv.shape[2:]),
-        tcol,
-        sidx[0],
-        smask[0],
-        cot.reshape(tc, sensors),
-    )
+    )(*ins)
+    results = (out, gser, gconv, gmix)
+    out, gser, gconv, gmix = pl.pallas_call(
+        store_kernel,
+        out_shape=tuple(jax.ShapeDtypeStruct(x.shape, x.dtype) for x in results),
+        in_specs=[hb] * 4,
+        out_specs=(hb,) * 4,
+        scratch_shapes=[dma((4,))],
+    )(*results)
+    gconv = jnp.swapaxes(gconv, 2, 3)
     return out.reshape(series.shape), gser.reshape(series.shape), gconv, gmix
 
 

time: 72.4 us -> 79.7 us (1.10)
  Pallas kernels: 64.4 us -> 78.9 us
  local copies, waits for them, and re-layouts: 7.05 us -> 0 us
    pallas_call x0 -> x1, Pallas kernels: none -> 16 us  [per_device(): pl.pallas_call(store_kernel, out_shape=tuple((jax.ShapeDtypeStruct(x.shap...]
    unnamed x23 -> x0, local copies, waits for them, and re-layouts: 7.05 us -> none
    pallas_call x1, Pallas kernels: 64.4 us -> 62.8 us  [per_device(): pl.pallas_call(functools.partial(kernel, n_graph, n_tm, steps, scale), ou...]
where the time goes in v2:
time: 79.7 us; the launch traced here: 79.5 us
  Pallas kernels  78.9 us (99%)
    pallas_call x1, Pallas kernels, per_device(): pl.pallas_call(functools.partial(kernel, n_graph, n_tm, steps, scale), ou...  62.8 us
    pallas_call x1, Pallas kernels, per_device(): pl.pallas_call(store_kernel, out_shape=tuple((jax.ShapeDtypeStruct(x.shap...  16 us

profile of v2, /device:TPU:0, one launch (start us, length us, event | category | flops | bytes accessed | tf_op | source)
XLA Modules:
  0.0 79.5 jit_solution(14744160148258714730)
XLA Ops:
  0.6 62.8 %shard_map.129 = (bf16[128,512]{1,0:T(8,128)(2,1)}, bf16[128,512]{1,0:T(8,128)(2,1)}, f32[2,2,32,64]{3,2,1,0:T(8,128)}, f32[2,5,32,32]{3,2,1,0:T(8,128)}) custom-call(bf16[128,512]{1,0:T(8,128)(2,1)} %bitcast.13, bf16[128,64]{1,0:T(8,128)(2,1)} %bitcast.16, f32[2,64]{1,0:T(2,128)} %cb_h.1, bf16[320,32]{1,0:T(8,128)(2,1)} %bitcast.15, f32[2,32]{1,0:T(2,128)} %mb_h.1, ...), custom_call_target="tpu_custom_call" | custom-call | tf_op jit(solution)/shard_map/pallas_call | solution.py:516
  63.5 16.0 %shard_map.130 = (bf16[128,512]{1,0:T(8,128)(2,1)}, bf16[128,512]{1,0:T(8,128)(2,1)}, f32[2,2,32,64]{3,2,1,0:T(8,128)}, f32[2,5,32,32]{3,2,1,0:T(8,128)}) custom-call(bf16[128,512]{1,0:T(8,128)(2,1)} %get-tuple-element.12.a, bf16[128,512]{1,0:T(8,128)(2,1)} %get-tuple-element.13.b, f32[2,2,32,64]{3,2,1,0:T(8,128)} %get-tuple-element.14.c, ...), custom_call_target="tpu_custom_call" | custom-call | tf_op jit(solution)/shard_map/pallas_call | solution.py:568

commit v3 on v2

--- a/solution.py
+++ b/solution.py
@@ -29,7 +29,7 @@
 
 def peers(count, body):
     if count <= 8:
-        for off in range(1, count):
+        for off in range(count - 1, 0, -1):
             body(off)
     elif count > 1:
         lax.fori_loop(1, count, lambda off, c: (body(off), c)[1], 0)
@@ -57,6 +57,17 @@
     lblocks = sensors // tile
     hblocks = halo // tile
     wire = send.dtype
+
+    def partner(off):
+        if n_graph & (n_graph - 1) or n_graph > 8:
+            return lax.rem(me + off, n_graph)
+        p = 0
+        bit = 1
+        while bit < n_graph:
+            p = p + lax.rem(me // bit + off // bit, 2) * bit
+            bit *= 2
+        return p
+
     er = e_part.shape[1]
 
     loads = [
@@ -71,7 +82,7 @@
     barrier = pltpu.get_barrier_semaphore()
 
     def greet_graph(off):
-        pl.semaphore_signal(barrier, inc=1, device_id={"graph": lax.rem(me + off, n_graph)}, device_id_type=MESH)
+        pl.semaphore_signal(barrier, inc=1, device_id={"graph": partner(off)}, device_id_type=MESH)
 
     def greet_tm(off):
         pl.semaphore_signal(barrier, inc=1, device_id={"tm": lax.rem(z + off, n_tm)}, device_id_type=MESH)
@@ -204,7 +215,7 @@
         send[r, :, 1] = sb.reshape(n_graph, slots, tc).astype(wire)
 
         def go(off):
-            p = lax.rem(me + off, n_graph)
+            p = partner(off)
             graph_copy(send.at[r, p], recv.at[r, me], r_ssem.at[r, p], r_rsem.at[r, me], p).start()
 
         peers(n_graph, go)
@@ -214,7 +225,7 @@
         filler()
 
         def take(off):
-            p = lax.rem(me + off, n_graph)
+            p = partner(off)
             graph_copy(send.at[r, p], recv.at[r, p], r_ssem.at[r, p], r_rsem.at[r, p], p).wait_recv()
 
         peers(n_graph, take)
@@ -362,7 +373,7 @@
                     e_part[p] = early[p * er:(p + 1) * er]
 
                 def scatter(off):
-                    p = lax.rem(me + off, n_graph)
+                    p = partner(off)
                     graph_copy(e_part.at[p], e_buf.at[me], e_ssem.at[p], e_rsem.at[me], p).start()
 
                 peers(n_graph, scatter)
@@ -433,7 +444,7 @@
         gconv[l, 1] = pltpu.roll(x, tc - 2 * ch, 1)[:, :2 * ch]
 
     def take_group(off):
-        p = lax.rem(me + off, n_graph)
+        p = partner(off)
         graph_copy(eg_buf.at[p], eg_buf.at[p], eg_ssem.at[p], eg_rsem.at[p], p).wait_recv()
 
     peers(n_graph, take_group)
@@ -447,7 +458,7 @@
     put_conv(0, gather_sum(lt_buf, lt_ssem, lt_rsem, n_tm, z, tm_copy) * scale)
 
     def sent_graph(off):
-        p = lax.rem(me + off, n_graph)
+        p = partner(off)
         for r in range(4 * GATED_LAYERS):
             graph_copy(send.at[r, p], recv.at[r, me], r_ssem.at[r, p], r_rsem.at[r, me], p).wait_send()
         graph_copy(e_part.at[p], e_buf.at[me], e_ssem.at[p], e_rsem.at[me], p).wait_send()
@@ -474,15 +485,11 @@
         shift_copy(3, pack_s.at[2], pack_r.at[2], -1).wait_send()
 
 
-def store_kernel(a, b, c, d, ao, bo, co, do, sem):
-    copies = [
-        pltpu.make_async_copy(src, dst, sem.at[i])
-        for i, (src, dst) in enumerate(((a, ao), (b, bo), (c, co), (d, do)))
-    ]
-    for copy in copies:
-        copy.start()
-    for copy in copies:
-        copy.wait()
+def store_kernel(a, b, c, d, ao, bo, co, do):
+    ao[...] = a[...]
+    bo[...] = b[...]
+    co[...] = c[...]
+    do[...] = d[...]
 
 
 def per_device(series, cw, cb, mw, mb, tv, tcol, sidx, smask, cot):
@@ -568,9 +575,8 @@
     out, gser, gconv, gmix = pl.pallas_call(
         store_kernel,
         out_shape=tuple(jax.ShapeDtypeStruct(x.shape, x.dtype) for x in results),
-        in_specs=[hb] * 4,
-        out_specs=(hb,) * 4,
-        scratch_shapes=[dma((4,))],
+        in_specs=[vm] * 4,
+        out_specs=(vm,) * 4,
     )(*results)
     gconv = jnp.swapaxes(gconv, 2, 3)
     return out.reshape(series.shape), gser.reshape(series.shape), gconv, gmix

time: 79.7 us -> 65.1 us (0.82)
  Pallas kernels: 78.9 us -> 64.3 us
    pallas_call x1, Pallas kernels: 16 us -> 1.86 us  [per_device(): pl.pallas_call(store_kernel, out_shape=tuple((jax.ShapeDtypeStruct(x.shap...]
where the time goes in v3:
time: 65.1 us; the launch traced here: 65 us
  Pallas kernels  64.3 us (99%)
    pallas_call x1, Pallas kernels, per_device(): pl.pallas_call(functools.partial(kernel, n_graph, n_tm, steps, scale), ou...  62.5 us
    pallas_call x1, Pallas kernels, per_device(): pl.pallas_call(store_kernel, out_shape=tuple((jax.ShapeDtypeStruct(x.shap...  1.86 us

profile of v3, /device:TPU:0, one launch (start us, length us, event | category | flops | bytes accessed | tf_op | source)
XLA Modules:
  0.0 65.0 jit_solution(2340585373145229108)
XLA Ops:
  0.6 62.5 %shard_map.129 = (bf16[128,512]{1,0:T(8,128)(2,1)}, bf16[128,512]{1,0:T(8,128)(2,1)}, f32[2,2,32,64]{3,2,1,0:T(8,128)}, f32[2,5,32,32]{3,2,1,0:T(8,128)}) custom-call(bf16[128,512]{1,0:T(8,128)(2,1)} %bitcast.13, bf16[128,64]{1,0:T(8,128)(2,1)} %bitcast.16, f32[2,64]{1,0:T(2,128)} %cb_h.1, bf16[320,32]{1,0:T(8,128)(2,1)} %bitcast.15, f32[2,32]{1,0:T(2,128)} %mb_h.1, ...), custom_call_target="tpu_custom_call" | custom-call | tf_op jit(solution)/shard_map/pallas_call | solution.py:523
  63.1 1.9 %shard_map.130 = (bf16[128,512]{1,0:T(8,128)(2,1)}, bf16[128,512]{1,0:T(8,128)(2,1)}, f32[2,2,32,64]{3,2,1,0:T(8,128)}, f32[2,5,32,32]{3,2,1,0:T(8,128)}) custom-call(bf16[128,512]{1,0:T(8,128)(2,1)} %get-tuple-element.12.a, bf16[128,512]{1,0:T(8,128)(2,1)} %get-tuple-element.13.b, f32[2,2,32,64]{3,2,1,0:T(8,128)} %get-tuple-element.14.c, ...), custom_call_target="tpu_custom_call" | custom-call | tf_op jit(solution)/shard_map/pallas_call | solution.py:575

commit v4 on v3

--- a/solution.py
+++ b/solution.py
@@ -25,6 +25,14 @@
 
 def dot_tn(a, b):
     return lax.dot_general(a, b, (((0,), (0,)), ((), ())), preferred_element_type=F32)
+
+
+def quot(x, n):
+    return x >> (n.bit_length() - 1) if n & (n - 1) == 0 else x // n
+
+
+def rest_of(x, n):
+    return x & (n - 1) if n & (n - 1) == 0 else lax.rem(x, n)
 
 
 def peers(count, body):
@@ -104,10 +112,11 @@
 
     row32 = lax.broadcasted_iota(jnp.int32, (ch, tc), 0)
     lane32 = lax.broadcasted_iota(jnp.int32, (ch, tc), 1)
-    spread = jnp.where(lax.rem(lane32, ch) == row32, 1.0, 0.0)
+    spread = jnp.where(rest_of(lane32, ch) == row32, 1.0, 0.0)
     spread_b = spread.astype(BF)
-    rt = lax.broadcasted_iota(jnp.int32, (tc, tc), 0) // ch
-    lt = lax.broadcasted_iota(jnp.int32, (tc, tc), 1) // ch
+    rt = lax.broadcasted_iota(jnp.int32, (tc, tc), 0)
+    lt = lax.broadcasted_iota(jnp.int32, (tc, tc), 1)
+    rt, lt = quot(rt, ch), quot(lt, ch)
     same = rt == lt
 
     def before(d):
@@ -121,7 +130,7 @@
     taps = 2 * GATED_LAYERS
     rs = lax.broadcasted_iota(jnp.int32, (taps * ch, taps * tc), 0)
     ls = lax.broadcasted_iota(jnp.int32, (taps * ch, taps * tc), 1)
-    spread_taps = jnp.where((ls // tc) * ch + lax.rem(ls, ch) == rs, 1.0, 0.0).astype(BF)
+    spread_taps = jnp.where(quot(ls, tc) * ch + rest_of(ls, ch) == rs, 1.0, 0.0).astype(BF)
     def after(d):
         return rt == lt - d
 
@@ -148,7 +157,7 @@
 
     r64 = lax.broadcasted_iota(jnp.int32, (2 * ch, 2 * tc), 0)
     l64 = lax.broadcasted_iota(jnp.int32, (2 * ch, 2 * tc), 1)
-    spread2 = jnp.where(lax.rem(l64, ch) + (l64 // tc) * ch == r64, 1.0, 0.0)
+    spread2 = jnp.where(rest_of(l64, ch) + quot(l64, tc) * ch == r64, 1.0, 0.0)
     cbias = lax.dot_general(cb[...], spread2, (((1,), (0,)), ((), ())), precision=lax.Precision.HIGHEST, preferred_element_type=F32)
     mbias = lax.dot_general(mb[...], spread, (((1,), (0,)), ((), ())), precision=lax.Precision.HIGHEST, preferred_element_type=F32)
 
@@ -183,11 +192,11 @@
     key = jnp.where(smask[...] != 0, sidx[...] + 1, 0)
     es = lax.broadcasted_iota(jnp.int32, (slots, halo), 0)
     ej = lax.broadcasted_iota(jnp.int32, (slots, halo), 1)
-    pick = jnp.where(lax.rem(ej, slots) == es, 1.0, 0.0).astype(BF)
-    hi = dot((key // 32).astype(F32).astype(BF), pick)
-    lo = dot(lax.rem(key, 32).astype(F32).astype(BF), pick)
+    pick = jnp.where(rest_of(ej, slots) == es, 1.0, 0.0).astype(BF)
+    hi = dot((key >> 5).astype(F32).astype(BF), pick)
+    lo = dot((key & 31).astype(F32).astype(BF), pick)
     pr = lax.broadcasted_iota(jnp.int32, (n_graph, halo), 0)
-    pj = lax.broadcasted_iota(jnp.int32, (n_graph, halo), 1) // slots
+    pj = quot(lax.broadcasted_iota(jnp.int32, (n_graph, halo), 1), slots)
     keys = jnp.sum(jnp.where(pr == pj, hi * 32.0 + lo, 0.0), axis=0, keepdims=True)
     ids = lax.broadcasted_iota(jnp.int32, (sensors, halo), 0).astype(F32) + 1.0
     onehot = jnp.where(ids == keys, 1.0, 0.0)
@@ -216,7 +225,7 @@
 
         def go(off):
             p = partner(off)
-            graph_copy(send.at[r, p], recv.at[r, me], r_ssem.at[r, p], r_rsem.at[r, me], p).start()
+            graph_copy(send.at[r, p], recv.at[r, me], r_ssem.at[r, p], r_rsem.at[r], p).start()
 
         peers(n_graph, go)
         recv[r, me] = send[r, me]
@@ -224,13 +233,10 @@
         pushed = dot(wlt[...], push_in)
         filler()
 
-        def take(off):
-            p = partner(off)
-            graph_copy(send.at[r, p], recv.at[r, p], r_ssem.at[r, p], r_rsem.at[r, p], p).wait_recv()
-
-        peers(n_graph, take)
-        rp = recv[r, :, 0].astype(F32).reshape(halo, tc).astype(BF)
-        rb = recv[r, :, 1].astype(F32).reshape(halo, tc).astype(BF)
+        arrived = recv.at[r, pl.ds(0, n_graph - 1)]
+        graph_copy(arrived, arrived, r_ssem.at[r, 0], r_rsem.at[r], partner(1)).wait_recv()
+        rp = recv[r, :, 0].reshape(halo, tc).astype(BF)
+        rb = recv[r, :, 1].reshape(halo, tc).astype(BF)
         return pulled + dot(wh[...], rp), pushed + dot(gm[...], rb)
 
     lane_half = lax.broadcasted_iota(jnp.int32, (half_s, tc), 1) < tc // 2
@@ -309,7 +315,7 @@
 
     flow[...] = ctr[...]
 
-    lane_g = lax.broadcasted_iota(jnp.int32, (ch, tc), 1) // ch
+    lane_g = quot(lax.broadcasted_iota(jnp.int32, (ch, tc), 1), ch)
 
     def fold(x):
         y = x[0:ch]
@@ -460,7 +466,7 @@
     def sent_graph(off):
         p = partner(off)
         for r in range(4 * GATED_LAYERS):
-            graph_copy(send.at[r, p], recv.at[r, me], r_ssem.at[r, p], r_rsem.at[r, me], p).wait_send()
+            graph_copy(send.at[r, p], recv.at[r, me], r_ssem.at[r, p], r_rsem.at[r], p).wait_send()
         graph_copy(e_part.at[p], e_buf.at[me], e_ssem.at[p], e_rsem.at[me], p).wait_send()
         graph_copy(eg_buf.at[me], eg_buf.at[me], eg_ssem.at[p], eg_rsem.at[me], p).wait_send()
         graph_copy(l_buf.at[me], l_buf.at[me], l_ssem.at[p], l_rsem.at[me], p).wait_send()
@@ -559,7 +565,7 @@
             pltpu.VMEM((n_graph, er, tc), F32),
             *[pltpu.VMEM(x.shape, x.dtype) for x in ins[:6] + ins[7:]],
             dma((9,)),
-            dma((rounds, n_graph)), dma((rounds, n_graph)),
+            dma((rounds, n_graph)), dma((rounds,)),
             dma((4,)), dma((4,)),
             dma((n_graph,)), dma((n_graph,)),
             dma((n_tm,)), dma((n_tm,)),

time: 65.1 us -> 64.6 us (level)
  no operation moved by 1% of the time
where the time goes in v4:
time: 64.6 us; the launch traced here: 64.4 us
  Pallas kernels  63.8 us (99%)
    pallas_call x1, Pallas kernels, per_device(): pl.pallas_call(functools.partial(kernel, n_graph, n_tm, steps, scale), ou...  61.9 us
    pallas_call x1, Pallas kernels, per_device(): pl.pallas_call(store_kernel, out_shape=tuple((jax.ShapeDtypeStruct(x.shap...  1.86 us

profile of v4, /device:TPU:0, one launch (start us, length us, event | category | flops | bytes accessed | tf_op | source)
XLA Modules:
  0.0 64.4 jit_solution(15094247491385291203)
XLA Ops:
  0.6 61.9 %shard_map.129 = (bf16[128,512]{1,0:T(8,128)(2,1)}, bf16[128,512]{1,0:T(8,128)(2,1)}, f32[2,2,32,64]{3,2,1,0:T(8,128)}, f32[2,5,32,32]{3,2,1,0:T(8,128)}) custom-call(bf16[128,512]{1,0:T(8,128)(2,1)} %bitcast.13, bf16[128,64]{1,0:T(8,128)(2,1)} %bitcast.16, f32[2,64]{1,0:T(2,128)} %cb_h.1, bf16[320,32]{1,0:T(8,128)(2,1)} %bitcast.15, f32[2,32]{1,0:T(2,128)} %mb_h.1, ...), custom_call_target="tpu_custom_call" | custom-call | tf_op jit(solution)/shard_map/pallas_call | solution.py:529
  62.5 1.9 %shard_map.130 = (bf16[128,512]{1,0:T(8,128)(2,1)}, bf16[128,512]{1,0:T(8,128)(2,1)}, f32[2,2,32,64]{3,2,1,0:T(8,128)}, f32[2,5,32,32]{3,2,1,0:T(8,128)}) custom-call(bf16[128,512]{1,0:T(8,128)(2,1)} %get-tuple-element.12.a, bf16[128,512]{1,0:T(8,128)(2,1)} %get-tuple-element.13.b, f32[2,2,32,64]{3,2,1,0:T(8,128)} %get-tuple-element.14.c, ...), custom_call_target="tpu_custom_call" | custom-call | tf_op jit(solution)/shard_map/pallas_call | solution.py:581
